TPU v7x, 128 devices: a whole 4x4x4 slice. The times are simulated.
128 devices in a mesh: ep: 16 (over y, z_hi, core), dp: 8 (over z_lo, x).
Axes of the slice: x: 4, y: 4, z: 4 (z_hi: 2, z_lo: 2; z = z_hi * 2 + z_lo), core: 2. Of those that a mesh axis runs over, the one named last changes fastest.
Arguments:
- tokens: bfloat16 [8192, 2048], P(('ep', 'dp')), may hold values from -6 to 6
- slot_route: int32 [8192, 8], P(('ep', 'dp')), may hold values from 0 to 127, all different within a row; in each aligned block of 64 rows (0 to 63, 64 to 127, ...) at most 6 rows name the same one
- route_gate: float32 [8192, 8], P(('ep', 'dp')), may hold values from 0.04 to 0.4
- placement_table: int32 [128], replicated, may hold values from 0 to 63, as said below
- refreshed: int32 [32], replicated, may hold values from 0 to 63, as said below
- slot_gate_up: bfloat16 [128, 2048, 1536], P(('ep', 'dp')), may hold values from -0.125 to 0.125
- slot_down: bfloat16 [128, 768, 2048], P(('ep', 'dp')), may hold values from -0.21875 to 0.21875
- new_gate_up: bfloat16 [32, 2048, 1536], P('ep', 'dp'), may hold values from -0.125 to 0.125
- new_down: bfloat16 [32, 768, 2048], P('ep', 'dp'), may hold values from -0.21875 to 0.21875
Outputs:
- mixed: bfloat16 [8192, 2048], P(('ep', 'dp'))
Inputs may be any that keep to these rules, and one draw needn't show every extreme that they name: `placement_table`: slot s lives on device s of ep+dp (ep major); write s = c * 8 + m. Every expert has one slot or more. A slot with m < 6 serves a refreshed expert whose position r in refreshed has r // 2 = (c + f(m)) mod 16, where f(m) = m for m < 4, f(4) = 8 and f(5) = 15; a slot with m >= 6 serves an expert that is not refreshed. `refreshed`: distinct expert ids. `slot_route`: each row names 8 distinct slots. Among the 64 rows of one device no slot is named more than 6 times, a bound that some block reaches.
All inputs are finite; a program needn't handle non-finite values.
Results may differ from a plain program's by a relative error of at most 0.0057.
Values may be sent and summed in bfloat16 or wider, within the bound.
No kernel may reach another device: no remote copies, remote signals or barrier semaphores. Data moves between devices by JAX's collectives and lax.ppermute only.
A program may use at most 128 MiB of HBM per device.

v0:
```python
import jax
import jax.numpy as jnp
from jax import lax
from jax.experimental import pallas as pl
from jax.experimental.pallas import tpu as pltpu
from jax.sharding import Mesh
from jax.sharding import PartitionSpec as P


D = 2048
FF = 768
TOP = 8
CAP = 6
TOK = 64
SLOTS = 128
ACTIVE = 6
PACK = 8
WIDE = 1536
PART = 512
EP = ("y", "zh", "core")
DP = ("zl", "x")
EVERY = EP + DP
COLUMN = EP + ("zl",)
ROWS = SLOTS * PACK
DENSE = SLOTS * CAP


ANY = pl.BlockSpec(memory_space=pl.ANY)
SMEM = pl.BlockSpec(memory_space=pltpu.SMEM)
VMEM = pl.BlockSpec(memory_space=pltpu.VMEM)
F32 = jnp.float32
BF16 = jnp.bfloat16


def params():
    return pltpu.CompilerParams(vmem_limit_bytes=56 * 1024 * 1024)


def iota(shape, dim):
    return lax.broadcasted_iota(jnp.int32, shape, dim)


def nt_dot(a, b):
    return lax.dot_general(a, b, (((1,), (1,)), ((), ())), preferred_element_type=F32)


def nn_dot(a, b):
    return jnp.dot(a, b, preferred_element_type=F32)


def shift_of(member):
    return jnp.where(member < 4, member, jnp.where(member == 4, 8, jnp.where(member == 5, 15, 0)))


def home_of(slot):
    member = slot & 7
    return ((((slot >> 3) + shift_of(member)) & 15) << 3) | member


def pick_of(ids, table, refreshed, other):
    group = ids[0]
    slot = (((group - shift_of(other)) & 15) << 3) | other
    return (table[slot] == refreshed[2 * group + 1]).astype(jnp.int32)


def hits_of(home, k):
    return iota((SLOTS, TOK), 0) == home[k : k + 1, :]


def ranks(home):
    hits = jnp.zeros((SLOTS, TOK), F32)
    for k in range(TOP):
        hits = jnp.where(hits_of(home, k), 1.0, hits)
    before = (iota((TOK, TOK), 0) < iota((TOK, TOK), 1)).astype(F32).astype(BF16)
    rank = nn_dot(hits.astype(BF16), before)
    return jnp.where(hits > 0, rank, -1.0).astype(BF16)


def spread():
    return ((iota((ROWS, SLOTS), 0) >> 3) == iota((ROWS, SLOTS), 1)).astype(F32).astype(BF16)


def copy_all(pairs, sems):
    copies = [pltpu.make_async_copy(src, dst, sems.at[n]) for n, (src, dst) in enumerate(pairs)]
    for c in copies:
        c.start()
    for c in copies:
        c.wait()


def stage_kernel(ids, table, refreshed, *refs):
    count = (len(refs) - 5) // 2
    sources, outs, sem_in, sem_out = refs[:count], refs[count : count + 3], refs[-2], refs[-1]
    held = refs[count + 3 : -2]
    picks = [pick_of(ids, table, refreshed, ids[1] ^ k) for k in range(1, 4)]
    copy_all(list(zip(sources, held)), sem_in)
    copy_all(
        [
            (held[n].at[picks[k]], outs[k].at[n] if count > 1 else outs[k])
            for k in range(3)
            for n in range(count)
        ],
        sem_out,
    )


def dispatch_kernel(ids, *refs):
    packed, out = refs[:4], refs[4]
    column = ids[1] & 3
    lanes = iota((TOK, SLOTS), 1)
    lower = (iota((TOK, TOK), 0) > iota((TOK, TOK), 1)).astype(F32).astype(BF16)
    part = 32 * PACK
    every = (iota((part, SLOTS), 1) == 4 * (iota((part, SLOTS), 0) >> 3) + column).astype(F32)
    every = every.astype(BF16)
    place = (iota((part, SLOTS), 0) & 7).astype(F32)
    left = iota((part, SLOTS), 1) < TOK
    for k in range(4):
        home = home_of(packed[k][:, D:].astype(F32).astype(jnp.int32))
        hits = jnp.zeros((TOK, SLOTS), F32)
        for n in range(TOP):
            hits = jnp.where(home[:, n : n + 1] == lanes, 1.0, hits)
        rank = jnp.where(hits > 0, nn_dot(lower, hits.astype(BF16)), -1.0).astype(BF16)
        wide = nt_dot(every, jnp.concatenate([rank, rank], axis=0))
        main = left & (wide == place) & (place < CAP)
        for j in range(3):
            wanted = jnp.where(place == 6, float(j), jnp.where(place == 7, float(3 + j), -2.0))
            pick = (main | (jnp.logical_not(left) & (wide == wanted))).astype(F32).astype(BF16)
            cols = slice(PART * j, PART * (j + 1))
            rhs = jnp.concatenate([packed[k][:, cols], packed[k][:, WIDE:D]], axis=0)
            got = nn_dot(pick, rhs).reshape(32, PACK, PART)
            out[:, column ^ k, :, cols] = got.astype(BF16)


def compact_kernel(x, out):
    row = iota((96, 128), 0)
    col = iota((96, 128), 1)
    owner = row // 6
    rank = row - 6 * owner
    main = (col == 8 * owner + rank).astype(F32).astype(BF16)
    extra = []
    for j in range(3):
        hit = (col == 8 * owner + 6) & (rank == j) | (col == 8 * owner + 7) & (rank == 3 + j)
        extra.append(hit.astype(F32).astype(BF16))
    extra = jnp.concatenate(extra, axis=1)
    for b in range(8):
        blk = x[128 * b : 128 * (b + 1), :]
        out[96 * b : 96 * (b + 1), 0:WIDE] = nn_dot(main, blk).astype(BF16)
        tall = jnp.concatenate([blk[:, PART * j : PART * (j + 1)] for j in range(3)], axis=0)
        out[96 * b : 96 * (b + 1), WIDE:] = nn_dot(extra, tall).astype(BF16)


def up_kernel(ids, table, refreshed, x, own, swapped, *refs):
    got = refs[0:6]
    slot, out, wbuf, sem = refs[6:]
    member = ids[1]
    active = member < ACTIVE
    pick = pick_of(ids, table, refreshed, member)
    tile = 256

    def fetch(i):
        buf = i % 2

        @pl.when(active)
        def _():
            for side in range(2):
                cols = pl.ds(side * FF + tile * i, tile)
                for k in range(4):
                    for n in range(2):
                        if k == 0:
                            src = (own, swapped)[n].at[pick, :, cols]
                        else:
                            src = got[3 * n + k - 1].at[:, cols]
                        dst = wbuf.at[buf, side, pl.ds((member ^ (k + 4 * n)) * 256, 256), :]
                        pltpu.make_async_copy(src, dst, sem.at[buf]).start()

        @pl.when(jnp.logical_not(active))
        def _():
            for side in range(2):
                cols = pl.ds(side * FF + tile * i, tile)
                pltpu.make_async_copy(slot.at[0, :, cols], wbuf.at[buf, side], sem.at[buf]).start()

    fetch(0)
    for i in range(3):
        if i < 2:
            fetch(i + 1)
        pltpu.make_async_copy(wbuf.at[i % 2], wbuf.at[i % 2], sem.at[i % 2]).wait()
        gate = nn_dot(x[...], wbuf[i % 2, 0])
        up = nn_dot(x[...], wbuf[i % 2, 1])
        hidden = gate / (1.0 + jnp.exp(-gate)) * up
        out[:, tile * i : tile * (i + 1)] = hidden.astype(BF16)


def down_kernel(ids, table, refreshed, h, own, swapped, *refs):
    got = refs[0:3]
    slot, out, wbuf, sem = refs[3:]
    member = ids[1]
    active = member < ACTIVE
    pick = pick_of(ids, table, refreshed, member)

    @pl.when(active)
    def _():
        for k in range(4):
            for n in range(2):
                if k == 0:
                    src = (own, swapped)[n].at[pick]
                else:
                    src = got[k - 1].at[n]
                dst = wbuf.at[pl.ds((member ^ (k + 4 * n)) * 96, 96), :]
                pltpu.make_async_copy(src, dst, sem.at[0]).start()

    @pl.when(jnp.logical_not(active))
    def _():
        pltpu.make_async_copy(slot.at[0], wbuf, sem.at[0]).start()

    row = iota((128, 96), 0)
    col = iota((128, 96), 1)
    owner = row >> 3
    place = row & 7
    main = ((place < CAP) & (col == 6 * owner + place)).astype(F32).astype(BF16)
    extra = []
    for j in range(3):
        hit = (place == 6) & (col == 6 * owner + j) | (place == 7) & (col == 6 * owner + 3 + j)
        extra.append(hit.astype(F32).astype(BF16))
    pltpu.make_async_copy(wbuf, wbuf, sem.at[0]).wait()
    last = nn_dot(h[...], wbuf[:, WIDE:]).astype(BF16)
    for j in range(3):
        y = nn_dot(h[...], wbuf[:, PART * j : PART * (j + 1)]).astype(BF16)
        for b in range(8):
            rows = slice(96 * b, 96 * (b + 1))
            packed = nn_dot(main, y[rows]) + nn_dot(extra[j], last[rows])
            out[128 * b : 128 * (b + 1), PART * j : PART * (j + 1)] = packed.astype(BF16)


def weigh_kernel(route, gate, out):
    home = home_of(route[...])
    gates = jnp.zeros((SLOTS, TOK), F32)
    for k in range(TOP):
        gates = jnp.where(hits_of(home, k), gate[k : k + 1, :], gates)
    high = gates.astype(BF16)
    low = (gates - high.astype(F32)).astype(BF16)
    eye = (iota((TOK, TOK), 0) == iota((TOK, TOK), 1)).astype(F32).astype(BF16)
    every = spread()
    wide, high, low = [
        nt_dot(nt_dot(eye, v).astype(BF16), every) for v in (ranks(home), high, low)
    ]
    place = (iota((TOK, ROWS), 1) & 7).astype(F32)
    masks = [(wide == place) & (place < CAP)]
    for j in range(3):
        wanted = jnp.where(place == 6, float(j), jnp.where(place == 7, float(3 + j), -2.0))
        masks.append(wide == wanted)
    for i, mask in enumerate(masks):
        out[i, 0:TOK, :] = jnp.where(mask, high, 0.0).astype(BF16)
        out[i, TOK:, :] = jnp.where(mask, low, 0.0).astype(BF16)


def combine_kernel(weight, y, out):
    tail = jnp.zeros((TOK, PART), F32)
    for j in range(3):
        part = y[:, PART * j : PART * (j + 1)]
        stack = jnp.concatenate([weight[0], weight[1 + j]], axis=0)
        got = nn_dot(stack, part)
        out[:, PART * j : PART * (j + 1)] = (got[0:TOK] + got[TOK : 2 * TOK]).astype(BF16)
        tail = tail + (got[2 * TOK : 3 * TOK] + got[3 * TOK :])
    out[:, WIDE:] = tail.astype(BF16)


def resident(x):
    return pltpu.with_memory_space_constraint(x, pltpu.VMEM)


def shape(*dims, dtype=BF16):
    return jax.ShapeDtypeStruct(dims, dtype)


def per_device(
    tokens,
    slot_route,
    route_gate,
    placement_table,
    refreshed,
    slot_gate_up,
    slot_down,
    new_gate_up,
    new_down,
):
    ids = jnp.stack([lax.axis_index(EP), lax.axis_index(DP)]).astype(jnp.int32)
    where = (ids, placement_table, refreshed)
    route = slot_route.T
    gate = route_gate.T

    def swap(x):
        return lax.ppermute(x, "zl", [(0, 1), (1, 0)])

    def move(x, k):
        return lax.ppermute(x, DP, [(d ^ k, d) for d in range(ACTIVE)])

    def stage(dims, *sources):
        count = len(sources)
        held = [2] * (count > 1) + list(dims)
        return pl.pallas_call(
            stage_kernel,
            out_shape=[shape(*held)] * 3,
            in_specs=[SMEM] * 3 + [ANY] * count,
            out_specs=[ANY] * 3,
            scratch_shapes=[pltpu.VMEM((2, *dims), BF16)] * count
            + [pltpu.SemaphoreType.DMA((count,)), pltpu.SemaphoreType.DMA((3 * count,))],
            compiler_params=params(),
        )(*where, *sources)

    swapped_up = swap(new_gate_up)
    swapped_down = swap(new_down)
    marks = jnp.pad(slot_route.astype(BF16), ((0, 0), (0, 120)))
    packed = [jnp.concatenate([tokens, marks], axis=1)]
    for k in range(1, 4):
        packed.append(lax.ppermute(packed[0], "x", [(d ^ k, d) for d in range(4)]))
    own = stage((256, WIDE), new_gate_up)
    got_up = []
    for k in range(1, 4):
        got_up.append(move(own[k - 1], k))
    outgoing = pl.pallas_call(
        dispatch_kernel,
        out_shape=shape(32, 4, PACK, WIDE),
        in_specs=[SMEM] + [VMEM] * 4,
        out_specs=VMEM,
        compiler_params=params(),
        name="dispatch",
    )(ids, *[resident(p) for p in packed])
    incoming = lax.all_to_all(
        outgoing.reshape(32, 4 * PACK, WIDE), COLUMN, split_axis=0, concat_axis=0, tiled=True
    )
    incoming = resident(incoming.reshape(ROWS, WIDE))
    far = stage((256, WIDE), swapped_up)
    for k in range(1, 4):
        got_up.append(move(far[k - 1], k))
    both = stage((96, D), new_down, swapped_down)
    got_down = []
    for k in range(1, 4):
        got_down.append(move(both[k - 1], k))
    weight = pl.pallas_call(
        weigh_kernel,
        out_shape=shape(4, 2 * TOK, ROWS),
        in_specs=[VMEM, VMEM],
        out_specs=VMEM,
        compiler_params=params(),
        name="weigh",
    )(route, gate)
    rows = pl.pallas_call(
        compact_kernel,
        out_shape=shape(DENSE, D),
        in_specs=[VMEM],
        out_specs=VMEM,
        compiler_params=params(),
        name="compact",
    )(incoming)
    hidden = pl.pallas_call(
        up_kernel,
        out_shape=shape(DENSE, FF),
        in_specs=[SMEM] * 3 + [VMEM] + [ANY] * 9,
        out_specs=VMEM,
        scratch_shapes=[pltpu.VMEM((2, 2, D, 256), BF16), pltpu.SemaphoreType.DMA((2,))],
        compiler_params=params(),
        name="up",
    )(*where, rows, new_gate_up, swapped_up, *got_up, slot_gate_up)
    results = pl.pallas_call(
        down_kernel,
        out_shape=shape(ROWS, WIDE),
        in_specs=[SMEM] * 3 + [VMEM] + [ANY] * 6,
        out_specs=VMEM,
        scratch_shapes=[pltpu.VMEM((FF, D), BF16), pltpu.SemaphoreType.DMA((1,))],
        compiler_params=params(),
        name="down",
    )(*where, hidden, new_down, swapped_down, *got_down, slot_down)
    returned = lax.all_to_all(
        results.reshape(SLOTS, PACK, WIDE), EVERY, split_axis=0, concat_axis=0, tiled=True
    )
    returned = resident(returned.reshape(ROWS, WIDE))
    return pl.pallas_call(
        combine_kernel,
        out_shape=shape(TOK, D),
        in_specs=[VMEM, VMEM],
        out_specs=VMEM,
        compiler_params=params(),
        name="combine",
    )(weight, returned)


def solution(mesh):
    split = Mesh(mesh.devices.reshape(4, 2, 2, 2, 4), EVERY)
    return jax.shard_map(
        per_device,
        mesh=split,
        in_specs=(
            P(EVERY, None),
            P(EVERY, None),
            P(EVERY, None),
            P(),
            P(),
            P(EVERY, None, None),
            P(EVERY, None, None),
            P(EP, DP, None),
            P(EP, DP, None),
        ),
        out_specs=P(EVERY, None),
        check_vma=False,
    )
```

profile of v0, /device:TPU:1, one launch (start us, length us, event | category | flops | bytes accessed | tf_op | source)
XLA Modules:
  0.0 239.7 jit_solution(17102498971016042424)
XLA Ops:
  1.8 2.1 collective-permute-start
  3.9 2.5 %collective-permute-start.1 = (bf16[64,2176]{1,0:T(8,128)(2,1)S(1)}, bf16[64,2176]{1,0:T(8,128)(2,1)S(1)}, u32[]{:S(2)}, u32[]{:S(2)}) collective-permute-start(bf16[64,2176]{1,0:T(8,128)(2,1)S(1)} %fusion.1.refs_0_), channel_id=1, source_target_pairs={{2,0},{3,1},{0,2},{1,3},{6,4},{7,5},{4,6},{5,7},{10,8},{11,9},{8,1... | collective-permute-start | bytes 835592 | tf_op jit(solution)/shard_map/ppermute | solution.py:315
  6.4 1.8 collective-permute-start.3
  8.8 1.0 collective-permute-done.refs_1_
  9.8 8.6 %collective-permute-done.1.refs_2_ = bf16[64,2176]{1,0:T(8,128)(2,1)S(1)} collective-permute-done((bf16[64,2176]{1,0:T(8,128)(2,1)S(1)}, bf16[64,2176]{1,0:T(8,128)(2,1)S(1)}, u32[]{:S(2)}, u32[]{:S(2)}) %collective-permute-start.1) | collective-permute-done | bytes 278560 | tf_op jit(solution)/shard_map/ppermute | solution.py:315
  18.4 2.1 collective-permute-done.2.refs_3_
  20.5 5.0 %dispatch.1 = bf16[32,4,8,1536]{3,2,1,0:T(8,128)(2,1)} custom-call(s32[2]{0:T(128)} %pad_add_fusion.ids, bf16[64,2176]{1,0:T(8,128)(2,1)S(1)} %fusion.1.refs_0_, bf16[64,2176]{1,0:T(8,128)(2,1)S(1)} %collective-permute-done.refs_1_, bf16[64,2176]{1,0:T(8,128)(2,1)S(1)} %collective-permute-done.1.refs_2_, bf16[64,2176]{1,0:T(8,128)(2,1)S(1)} %collective-permute-done.2.refs_3_), custom_call_target="tpu_custom_call" | custom-call | tf_op jit(solution)/shard_map/dispatch/pallas_call | solution.py:320
  25.5 10.2 %all-to-all-start = ((bf16[32,32,1536]{2,1,0:T(8,128)(2,1)}), bf16[32,32,1536]{2,1,0:T(8,128)(2,1)S(1)}, u32[]{:S(2)}, u32[]{:S(2)}) async-start(bf16[32,32,1536]{2,1,0:T(8,128)(2,1)} %bitcast.10), calls=%async_computation | async-start | bytes 6291456 | tf_op jit(solution)/shard_map/all_to_all | solution.py:328
  35.7 1.4 collective-permute-start.10
  37.2 3.5 %shard_map.91 = (bf16[256,1536]{1,0:T(8,128)(2,1)}, bf16[256,1536]{1,0:T(8,128)(2,1)}, bf16[256,1536]{1,0:T(8,128)(2,1)}) custom-call(s32[2]{0:T(128)} %pad_add_fusion.ids, s32[128]{0:T(128)} %table.9, s32[32]{0:T(128)} %refreshed.9, bf16[2,256,1536]{2,1,0:T(8,128)(2,1)} %own.2), custom_call_target="tpu_custom_call" | custom-call | tf_op jit(solution)/shard_map/pallas_call | solution.py:300
  40.7 1.9 collective-permute-start.4
  42.6 3.3 %collective-permute-start.5 = (bf16[256,1536]{1,0:T(8,128)(2,1)}, bf16[256,1536]{1,0:T(8,128)(2,1)S(1)}, u32[]{:S(2)}, u32[]{:S(2)}) collective-permute-start(bf16[256,1536]{1,0:T(8,128)(2,1)} %get-tuple-element.15), channel_id=1, source_target_pairs={{2,0},{3,1},{0,2},{1,3},{6,4},{7,5},{10,8},{11,9},{8,10},{9,11},{1... | collective-permute-start | bytes 2359304 | tf_op jit(solution)/shard_map/ppermute | solution.py:295
  45.9 4.4 %collective-permute-start.6 = (bf16[256,1536]{1,0:T(8,128)(2,1)}, bf16[256,1536]{1,0:T(8,128)(2,1)S(1)}, u32[]{:S(2)}, u32[]{:S(2)}) collective-permute-start(bf16[256,1536]{1,0:T(8,128)(2,1)} %get-tuple-element.16), channel_id=1, source_target_pairs={{3,0},{2,1},{1,2},{0,3},{7,4},{6,5},{11,8},{10,9},{9,10},{8,11},{1... | collective-permute-start | bytes 2359304 | tf_op jit(solution)/shard_map/ppermute | solution.py:295
  50.3 3.5 %shard_map.92 = (bf16[256,1536]{1,0:T(8,128)(2,1)}, bf16[256,1536]{1,0:T(8,128)(2,1)}, bf16[256,1536]{1,0:T(8,128)(2,1)}) custom-call(s32[2]{0:T(128)} %pad_add_fusion.ids, s32[128]{0:T(128)} %table.9, s32[32]{0:T(128)} %refreshed.9, bf16[2,256,1536]{2,1,0:T(8,128)(2,1)} %collective-permute-done.3.refs_0_.swapped), custom_call_target="tpu_custom_call" | custom-call | tf_op jit(solution)/shard_map/pallas_call | solution.py:300
  53.8 1.9 collective-permute-start.7
  55.7 36.9 %collective-permute-done.10.refs_1_.swapped = bf16[2,96,2048]{2,1,0:T(8,128)(2,1)S(1)} collective-permute-done((bf16[2,96,2048]{2,1,0:T(8,128)(2,1)}, bf16[2,96,2048]{2,1,0:T(8,128)(2,1)S(1)}, u32[]{:S(2)}, u32[]{:S(2)}) %collective-permute-start.10) | collective-permute-done | bytes 786464 | tf_op jit(solution)/shard_map/ppermute | solution.py:292
  93.6 3.6 %shard_map.93 = (bf16[2,96,2048]{2,1,0:T(8,128)(2,1)}, bf16[2,96,2048]{2,1,0:T(8,128)(2,1)}, bf16[2,96,2048]{2,1,0:T(8,128)(2,1)}) custom-call(s32[2]{0:T(128)} %pad_add_fusion.ids, s32[128]{0:T(128)} %table.9, s32[32]{0:T(128)} %refreshed.9, bf16[2,96,2048]{2,1,0:T(8,128)(2,1)} %own.3, bf16[2,96,2048]{2,1,0:T(8,128)(2,1)} %copy-done), custom_call_target="tpu_custom_call" | custom-call | tf_op jit(solution)/shard_map/pallas_call | solution.py:300
  97.2 1.9 collective-permute-start.11
  99.1 5.0 %collective-permute-start.8 = (bf16[256,1536]{1,0:T(8,128)(2,1)}, bf16[256,1536]{1,0:T(8,128)(2,1)}, u32[]{:S(2)}, u32[]{:S(2)}) collective-permute-start(bf16[256,1536]{1,0:T(8,128)(2,1)} %get-tuple-element.18), channel_id=1, source_target_pairs={{2,0},{3,1},{0,2},{1,3},{6,4},{7,5},{10,8},{11,9},{8,10},{9,11},{1... | collective-permute-start | bytes 2359304 | tf_op jit(solution)/shard_map/ppermute | solution.py:295
  104.1 2.7 %collective-permute-start.9 = (bf16[256,1536]{1,0:T(8,128)(2,1)}, bf16[256,1536]{1,0:T(8,128)(2,1)}, u32[]{:S(2)}, u32[]{:S(2)}) collective-permute-start(bf16[256,1536]{1,0:T(8,128)(2,1)} %get-tuple-element.19), channel_id=1, source_target_pairs={{3,0},{2,1},{1,2},{0,3},{7,4},{6,5},{11,8},{10,9},{9,10},{8,11},{1... | collective-permute-start | bytes 2359304 | tf_op jit(solution)/shard_map/ppermute | solution.py:295
  106.8 2.3 collective-permute-start.12
  110.1 3.6 %collective-permute-start.13 = (bf16[2,96,2048]{2,1,0:T(8,128)(2,1)}, bf16[2,96,2048]{2,1,0:T(8,128)(2,1)}, u32[]{:S(2)}, u32[]{:S(2)}) collective-permute-start(bf16[2,96,2048]{2,1,0:T(8,128)(2,1)} %get-tuple-element.22), channel_id=1, source_target_pairs={{3,0},{2,1},{1,2},{0,3},{7,4},{6,5},{11,8},{10,9},{9,10},{8,11},{1... | collective-permute-start | bytes 2359304 | tf_op jit(solution)/shard_map/ppermute | solution.py:295
  113.7 3.0 %compact.1.x = bf16[768,2048]{1,0:T(8,128)(2,1)} custom-call(bf16[1024,1536]{1,0:T(8,128)(2,1)S(1)} %bitcast.8), custom_call_target="tpu_custom_call" | custom-call | tf_op jit(solution)/shard_map/compact/pallas_call | solution.py:347
  116.7 18.1 %collective-permute-done.8.refs_4_ = bf16[256,1536]{1,0:T(8,128)(2,1)} collective-permute-done((bf16[256,1536]{1,0:T(8,128)(2,1)}, bf16[256,1536]{1,0:T(8,128)(2,1)}, u32[]{:S(2)}, u32[]{:S(2)}) %collective-permute-start.8) | collective-permute-done | bytes 786464 | tf_op jit(solution)/shard_map/ppermute | solution.py:295
  134.8 22.8 %collective-permute-done.9.refs_5_ = bf16[256,1536]{1,0:T(8,128)(2,1)} collective-permute-done((bf16[256,1536]{1,0:T(8,128)(2,1)}, bf16[256,1536]{1,0:T(8,128)(2,1)}, u32[]{:S(2)}, u32[]{:S(2)}) %collective-permute-start.9) | collective-permute-done | bytes 786464 | tf_op jit(solution)/shard_map/ppermute | solution.py:295
  157.6 10.0 %up.1.h = bf16[768,768]{1,0:T(8,128)(2,1)} custom-call(s32[2]{0:T(128)} %pad_add_fusion.ids, s32[128]{0:T(128)} %table.9, s32[32]{0:T(128)} %refreshed.9, bf16[768,2048]{1,0:T(8,128)(2,1)} %compact.1.x, bf16[2,256,1536]{2,1,0:T(8,128)(2,1)} %own.2, bf16[2,256,1536]{2,1,0:T(8,128)(2,1)} %collective-permute-done.3.refs_0_.swapped, ...), custom_call_target="tpu_custom_call" | custom-call | tf_op jit(solution)/shard_map/up/pallas_call | solution.py:355
  167.7 6.8 %collective-permute-done.13.refs_2_ = bf16[2,96,2048]{2,1,0:T(8,128)(2,1)} collective-permute-done((bf16[2,96,2048]{2,1,0:T(8,128)(2,1)}, bf16[2,96,2048]{2,1,0:T(8,128)(2,1)}, u32[]{:S(2)}, u32[]{:S(2)}) %collective-permute-start.13) | collective-permute-done | bytes 786464 | tf_op jit(solution)/shard_map/ppermute | solution.py:295
  174.4 9.0 %down.1 = bf16[1024,1536]{1,0:T(8,128)(2,1)} custom-call(s32[2]{0:T(128)} %pad_add_fusion.ids, s32[128]{0:T(128)} %table.9, s32[32]{0:T(128)} %refreshed.9, bf16[768,768]{1,0:T(8,128)(2,1)} %up.1.h, bf16[2,96,2048]{2,1,0:T(8,128)(2,1)} %own.3, bf16[2,96,2048]{2,1,0:T(8,128)(2,1)} %copy-done, bf16[2,96,2048]{2,1,0:T(8,128)(2,1)} %collective-permute-done.11.refs_0_, ...), custom_call_target="tpu_custom_call" | custom-call | tf_op jit(solution)/shard_map/down/pallas_call | solution.py:364
  183.5 11.6 %all-to-all-start.1 = ((bf16[128,8,1536]{2,1,0:T(8,128)(2,1)}), bf16[128,8,1536]{2,1,0:T(8,128)(2,1)S(1)}, u32[]{:S(2)}, u32[]{:S(2)}) async-start(bf16[128,8,1536]{2,1,0:T(8,128)(2,1)} %bitcast.11), calls=%async_computation.1 | async-start | bytes 6291456 | tf_op jit(solution)/shard_map/all_to_all | solution.py:373
  195.1 2.7 %weigh.1.weight = bf16[4,128,1024]{2,1,0:T(8,128)(2,1)} custom-call(s32[8,64]{1,0:T(8,128)} %bitcast.12, f32[8,64]{1,0:T(8,128)} %bitcast.13), custom_call_target="tpu_custom_call" | custom-call | tf_op jit(solution)/shard_map/weigh/pallas_call | solution.py:339
  197.8 39.0 %all-to-all-done.1 = bf16[128,8,1536]{2,1,0:T(8,128)(2,1)S(1)} async-done(((bf16[128,8,1536]{2,1,0:T(8,128)(2,1)}), bf16[128,8,1536]{2,1,0:T(8,128)(2,1)S(1)}, u32[]{:S(2)}, u32[]{:S(2)}) %all-to-all-start.1) | async-done | bytes 3145760 | tf_op jit(solution)/shard_map/all_to_all | solution.py:373
  236.7 2.9 %combine.1 = bf16[64,2048]{1,0:T(8,128)(2,1)} custom-call(bf16[4,128,1024]{2,1,0:T(8,128)(2,1)} %weigh.1.weight, bf16[1024,1536]{1,0:T(8,128)(2,1)S(1)} %bitcast.9), custom_call_target="tpu_custom_call" | custom-call | tf_op jit(solution)/shard_map/combine/pallas_call | solution.py:377
  (23 shorter events, 4.2 us)
Async XLA Ops:
  1.8 8.1 %collective-permute-start = (bf16[64,2176]{1,0:T(8,128)(2,1)S(1)}, bf16[64,2176]{1,0:T(8,128)(2,1)S(1)}, u32[]{:S(2)}, u32[]{:S(2)}) collective-permute-start(bf16[64,2176]{1,0:T(8,128)(2,1)S(1)} %fusion.1.refs_0_), channel_id=1, source_target_pairs={{1,0},{0,1},{3,2},{2,3},{5,4},{4,5},{7,6},{6,7},{9,8},{8,9},{11,10... | collective-permute-start | bytes 835592 | tf_op jit(solution)/shard_map/ppermute | solution.py:315
  3.9 14.5 %collective-permute-start.1 = (bf16[64,2176]{1,0:T(8,128)(2,1)S(1)}, bf16[64,2176]{1,0:T(8,128)(2,1)S(1)}, u32[]{:S(2)}, u32[]{:S(2)}) collective-permute-start(bf16[64,2176]{1,0:T(8,128)(2,1)S(1)} %fusion.1.refs_0_), channel_id=1, source_target_pairs={{2,0},{3,1},{0,2},{1,3},{6,4},{7,5},{4,6},{5,7},{10,8},{11,9},{8,1... | collective-permute-start | bytes 835592 | tf_op jit(solution)/shard_map/ppermute | solution.py:315
  6.3 14.2 %collective-permute-start.2 = (bf16[64,2176]{1,0:T(8,128)(2,1)S(1)}, bf16[64,2176]{1,0:T(8,128)(2,1)S(1)}, u32[]{:S(2)}, u32[]{:S(2)}) collective-permute-start(bf16[64,2176]{1,0:T(8,128)(2,1)S(1)} %fusion.1.refs_0_), channel_id=1, source_target_pairs={{3,0},{2,1},{1,2},{0,3},{7,4},{6,5},{5,6},{4,7},{11,8},{10,9},{9,1... | collective-permute-start | bytes 835592 | tf_op jit(solution)/shard_map/ppermute | solution.py:315
  6.4 43.9 %collective-permute-start.3 = (bf16[2,256,1536]{2,1,0:T(8,128)(2,1)}, bf16[2,256,1536]{2,1,0:T(8,128)(2,1)}, u32[]{:S(2)}, u32[]{:S(2)}) collective-permute-start(bf16[2,256,1536]{2,1,0:T(8,128)(2,1)} %own.2), channel_id=1, source_target_pairs={{0,4},{4,0},{1,5},{5,1},{2,6},{6,2},{3,7},{7,3},{8,12},{12,8},{9,1... | collective-permute-start | bytes 4718600 | tf_op jit(solution)/shard_map/ppermute | solution.py:292
  25.5 88.2 %all-to-all-start = ((bf16[32,32,1536]{2,1,0:T(8,128)(2,1)}), bf16[32,32,1536]{2,1,0:T(8,128)(2,1)S(1)}, u32[]{:S(2)}, u32[]{:S(2)}) async-start(bf16[32,32,1536]{2,1,0:T(8,128)(2,1)} %bitcast.10), calls=%async_computation | async-start | bytes 6291456 | tf_op jit(solution)/shard_map/all_to_all | solution.py:328
  35.7 57.0 %collective-permute-start.10 = (bf16[2,96,2048]{2,1,0:T(8,128)(2,1)}, bf16[2,96,2048]{2,1,0:T(8,128)(2,1)S(1)}, u32[]{:S(2)}, u32[]{:S(2)}) collective-permute-start(bf16[2,96,2048]{2,1,0:T(8,128)(2,1)} %own.3), channel_id=1, source_target_pairs={{0,4},{4,0},{1,5},{5,1},{2,6},{6,2},{3,7},{7,3},{8,12},{12,8},{9,1... | collective-permute-start | bytes 2359304 | tf_op jit(solution)/shard_map/ppermute | solution.py:292
  40.7 58.4 %collective-permute-start.4 = (bf16[256,1536]{1,0:T(8,128)(2,1)}, bf16[256,1536]{1,0:T(8,128)(2,1)S(1)}, u32[]{:S(2)}, u32[]{:S(2)}) collective-permute-start(bf16[256,1536]{1,0:T(8,128)(2,1)} %get-tuple-element.14), channel_id=1, source_target_pairs={{1,0},{0,1},{3,2},{2,3},{5,4},{4,5},{9,8},{8,9},{11,10},{10,11},{1... | collective-permute-start | bytes 2359304 | tf_op jit(solution)/shard_map/ppermute | solution.py:295
  42.6 61.5 %collective-permute-start.5 = (bf16[256,1536]{1,0:T(8,128)(2,1)}, bf16[256,1536]{1,0:T(8,128)(2,1)S(1)}, u32[]{:S(2)}, u32[]{:S(2)}) collective-permute-start(bf16[256,1536]{1,0:T(8,128)(2,1)} %get-tuple-element.15), channel_id=1, source_target_pairs={{2,0},{3,1},{0,2},{1,3},{6,4},{7,5},{10,8},{11,9},{8,10},{9,11},{1... | collective-permute-start | bytes 2359304 | tf_op jit(solution)/shard_map/ppermute | solution.py:295
  45.9 60.9 %collective-permute-start.6 = (bf16[256,1536]{1,0:T(8,128)(2,1)}, bf16[256,1536]{1,0:T(8,128)(2,1)S(1)}, u32[]{:S(2)}, u32[]{:S(2)}) collective-permute-start(bf16[256,1536]{1,0:T(8,128)(2,1)} %get-tuple-element.16), channel_id=1, source_target_pairs={{3,0},{2,1},{1,2},{0,3},{7,4},{6,5},{11,8},{10,9},{9,10},{8,11},{1... | collective-permute-start | bytes 2359304 | tf_op jit(solution)/shard_map/ppermute | solution.py:295
  53.8 55.4 %collective-permute-start.7 = (bf16[256,1536]{1,0:T(8,128)(2,1)}, bf16[256,1536]{1,0:T(8,128)(2,1)S(1)}, u32[]{:S(2)}, u32[]{:S(2)}) collective-permute-start(bf16[256,1536]{1,0:T(8,128)(2,1)} %get-tuple-element.17), channel_id=1, source_target_pairs={{1,0},{0,1},{3,2},{2,3},{5,4},{4,5},{9,8},{8,9},{11,10},{10,11},{1... | collective-permute-start | bytes 2359304 | tf_op jit(solution)/shard_map/ppermute | solution.py:295
  92.7 0.9 copy-start
  97.2 70.5 %collective-permute-start.11 = (bf16[2,96,2048]{2,1,0:T(8,128)(2,1)}, bf16[2,96,2048]{2,1,0:T(8,128)(2,1)}, u32[]{:S(2)}, u32[]{:S(2)}) collective-permute-start(bf16[2,96,2048]{2,1,0:T(8,128)(2,1)} %get-tuple-element.20), channel_id=1, source_target_pairs={{1,0},{0,1},{3,2},{2,3},{5,4},{4,5},{9,8},{8,9},{11,10},{10,11},{1... | collective-permute-start | bytes 2359304 | tf_op jit(solution)/shard_map/ppermute | solution.py:295
  99.1 10.1 %copy-start.1 = (bf16[256,1536]{1,0:T(8,128)(2,1)}, bf16[256,1536]{1,0:T(8,128)(2,1)S(1)}, u32[]{:S(2)}) copy-start(bf16[256,1536]{1,0:T(8,128)(2,1)S(1)} %collective-permute-done.4.refs_0_) | copy-start | bytes 2359300
  99.1 35.7 %collective-permute-start.8 = (bf16[256,1536]{1,0:T(8,128)(2,1)}, bf16[256,1536]{1,0:T(8,128)(2,1)}, u32[]{:S(2)}, u32[]{:S(2)}) collective-permute-start(bf16[256,1536]{1,0:T(8,128)(2,1)} %get-tuple-element.18), channel_id=1, source_target_pairs={{2,0},{3,1},{0,2},{1,3},{6,4},{7,5},{10,8},{11,9},{8,10},{9,11},{1... | collective-permute-start | bytes 2359304 | tf_op jit(solution)/shard_map/ppermute | solution.py:295
  104.1 5.1 %copy-start.2 = (bf16[256,1536]{1,0:T(8,128)(2,1)}, bf16[256,1536]{1,0:T(8,128)(2,1)S(1)}, u32[]{:S(2)}) copy-start(bf16[256,1536]{1,0:T(8,128)(2,1)S(1)} %collective-permute-done.5.refs_1_) | copy-start | bytes 2359300
  104.1 53.5 %collective-permute-start.9 = (bf16[256,1536]{1,0:T(8,128)(2,1)}, bf16[256,1536]{1,0:T(8,128)(2,1)}, u32[]{:S(2)}, u32[]{:S(2)}) collective-permute-start(bf16[256,1536]{1,0:T(8,128)(2,1)} %get-tuple-element.19), channel_id=1, source_target_pairs={{3,0},{2,1},{1,2},{0,3},{7,4},{6,5},{11,8},{10,9},{9,10},{8,11},{1... | collective-permute-start | bytes 2359304 | tf_op jit(solution)/shard_map/ppermute | solution.py:295
  106.8 2.4 copy-start.3
  106.8 60.8 %collective-permute-start.12 = (bf16[2,96,2048]{2,1,0:T(8,128)(2,1)}, bf16[2,96,2048]{2,1,0:T(8,128)(2,1)}, u32[]{:S(2)}, u32[]{:S(2)}) collective-permute-start(bf16[2,96,2048]{2,1,0:T(8,128)(2,1)} %get-tuple-element.21), channel_id=1, source_target_pairs={{2,0},{3,1},{0,2},{1,3},{6,4},{7,5},{10,8},{11,9},{8,10},{9,11},{1... | collective-permute-start | bytes 2359304 | tf_op jit(solution)/shard_map/ppermute | solution.py:295
  109.2 0.9 copy-start.4
  110.1 64.4 %collective-permute-start.13 = (bf16[2,96,2048]{2,1,0:T(8,128)(2,1)}, bf16[2,96,2048]{2,1,0:T(8,128)(2,1)}, u32[]{:S(2)}, u32[]{:S(2)}) collective-permute-start(bf16[2,96,2048]{2,1,0:T(8,128)(2,1)} %get-tuple-element.22), channel_id=1, source_target_pairs={{3,0},{2,1},{1,2},{0,3},{7,4},{6,5},{11,8},{10,9},{9,10},{8,11},{1... | collective-permute-start | bytes 2359304 | tf_op jit(solution)/shard_map/ppermute | solution.py:295
  183.5 53.3 %all-to-all-start.1 = ((bf16[128,8,1536]{2,1,0:T(8,128)(2,1)}), bf16[128,8,1536]{2,1,0:T(8,128)(2,1)S(1)}, u32[]{:S(2)}, u32[]{:S(2)}) async-start(bf16[128,8,1536]{2,1,0:T(8,128)(2,1)} %bitcast.11), calls=%async_computation.1 | async-start | bytes 6291456 | tf_op jit(solution)/shard_map/all_to_all | solution.py:373
where the time goes:
time: 240 us
  waiting for transfers between devices  135 us (56%)
  starting transfers between devices  56.7 us (24%)
  Pallas kernels  43.2 us (18%)
    ppermute x9, waiting for transfers between devices, move(): return lax.ppermute(x, DP, [(d ^ k, d) for d in range(ACTIVE)])  47.7 us
    all_to_all x1, waiting for transfers between devices, per_device(): lax.all_to_all(results.reshape(SLOTS, PACK, WIDE), EVERY, split_axis=0, c...  39 us
    ppermute x2, waiting for transfers between devices, swap(): return lax.ppermute(x, 'zl', [(0, 1), (1, 0)])  36.9 us
    ppermute x9, starting transfers between devices, move(): return lax.ppermute(x, DP, [(d ^ k, d) for d in range(ACTIVE)])  27 us
    ppermute x3, waiting for transfers between devices, per_device(): packed.append(lax.ppermute(packed[0], 'x', [(d ^ k, d) for d in range(4)]))  11.7 us
    all_to_all x1, starting transfers between devices, per_device(): lax.all_to_all(results.reshape(SLOTS, PACK, WIDE), EVERY, split_axis=0, c...  11.6 us
    pallas_call x3, Pallas kernels, stage(): pl.pallas_call(stage_kernel, out_shape=[shape(*held)] * 3, in_specs=[SMEM...  10.6 us
    all_to_all x1, starting transfers between devices, per_device(): lax.all_to_all(outgoing.reshape(32, 4 * PACK, WIDE), COLUMN, split_axis=0...  10.2 us
  transfers between devices with their start and end apart: 16, of which 8 were waited for; matrix products, arithmetic and copies ran while one was open for 0% of the time, Pallas kernels for 13%

commit v1 on v0

--- a/solution.py
+++ b/solution.py
@@ -25,15 +25,15 @@
 DENSE = SLOTS * CAP
 
 
-ANY = pl.BlockSpec(memory_space=pl.ANY)
+HBM = pl.BlockSpec(memory_space=pltpu.HBM)
 SMEM = pl.BlockSpec(memory_space=pltpu.SMEM)
 VMEM = pl.BlockSpec(memory_space=pltpu.VMEM)
 F32 = jnp.float32
 BF16 = jnp.bfloat16
 
 
-def params():
-    return pltpu.CompilerParams(vmem_limit_bytes=56 * 1024 * 1024)
+def params(mib=20):
+    return pltpu.CompilerParams(vmem_limit_bytes=mib * 1024 * 1024)
 
 
 def iota(shape, dim):
@@ -134,19 +134,23 @@
 def compact_kernel(x, out):
     row = iota((96, 128), 0)
     col = iota((96, 128), 1)
-    owner = row // 6
-    rank = row - 6 * owner
-    main = (col == 8 * owner + rank).astype(F32).astype(BF16)
+    rank = row >> 4
+    base = (row & 15) * 8
+    main = (col == base + rank).astype(F32).astype(BF16)
     extra = []
     for j in range(3):
-        hit = (col == 8 * owner + 6) & (rank == j) | (col == 8 * owner + 7) & (rank == 3 + j)
+        hit = (col == base + 6) & (rank == j) | (col == base + 7) & (rank == 3 + j)
         extra.append(hit.astype(F32).astype(BF16))
     extra = jnp.concatenate(extra, axis=1)
     for b in range(8):
         blk = x[128 * b : 128 * (b + 1), :]
-        out[96 * b : 96 * (b + 1), 0:WIDE] = nn_dot(main, blk).astype(BF16)
+        head = nn_dot(main, blk).astype(BF16)
         tall = jnp.concatenate([blk[:, PART * j : PART * (j + 1)] for j in range(3)], axis=0)
-        out[96 * b : 96 * (b + 1), WIDE:] = nn_dot(extra, tall).astype(BF16)
+        tail = nn_dot(extra, tall).astype(BF16)
+        for r in range(CAP):
+            rows = slice(128 * r + 16 * b, 128 * r + 16 * (b + 1))
+            out[rows, 0:WIDE] = head[16 * r : 16 * (r + 1)]
+            out[rows, WIDE:] = tail[16 * r : 16 * (r + 1)]
 
 
 def up_kernel(ids, table, refreshed, x, own, swapped, *refs):
@@ -192,43 +196,52 @@
 
 def down_kernel(ids, table, refreshed, h, own, swapped, *refs):
     got = refs[0:3]
-    slot, out, wbuf, sem = refs[3:]
+    slot, out, wbuf, wide, packed, sem, sem_out = refs[3:]
+    sends = []
     member = ids[1]
     active = member < ACTIVE
     pick = pick_of(ids, table, refreshed, member)
+    order = (3, 0, 1, 2)
 
     @pl.when(active)
     def _():
-        for k in range(4):
-            for n in range(2):
-                if k == 0:
-                    src = (own, swapped)[n].at[pick]
-                else:
-                    src = got[k - 1].at[n]
-                dst = wbuf.at[pl.ds((member ^ (k + 4 * n)) * 96, 96), :]
-                pltpu.make_async_copy(src, dst, sem.at[0]).start()
+        for j in order:
+            cols = pl.ds(PART * j, PART)
+            for k in range(4):
+                for n in range(2):
+                    if k == 0:
+                        src = (own, swapped)[n].at[pick, :, cols]
+                    else:
+                        src = got[k - 1].at[n, :, cols]
+                    dst = wbuf.at[j, pl.ds((member ^ (k + 4 * n)) * 96, 96), :]
+                    pltpu.make_async_copy(src, dst, sem.at[j]).start()
 
     @pl.when(jnp.logical_not(active))
     def _():
-        pltpu.make_async_copy(slot.at[0], wbuf, sem.at[0]).start()
-
-    row = iota((128, 96), 0)
-    col = iota((128, 96), 1)
-    owner = row >> 3
-    place = row & 7
-    main = ((place < CAP) & (col == 6 * owner + place)).astype(F32).astype(BF16)
-    extra = []
-    for j in range(3):
-        hit = (place == 6) & (col == 6 * owner + j) | (place == 7) & (col == 6 * owner + 3 + j)
-        extra.append(hit.astype(F32).astype(BF16))
-    pltpu.make_async_copy(wbuf, wbuf, sem.at[0]).wait()
-    last = nn_dot(h[...], wbuf[:, WIDE:]).astype(BF16)
-    for j in range(3):
-        y = nn_dot(h[...], wbuf[:, PART * j : PART * (j + 1)]).astype(BF16)
-        for b in range(8):
-            rows = slice(96 * b, 96 * (b + 1))
-            packed = nn_dot(main, y[rows]) + nn_dot(extra[j], last[rows])
-            out[128 * b : 128 * (b + 1), PART * j : PART * (j + 1)] = packed.astype(BF16)
+        for j in order:
+            cols = pl.ds(PART * j, PART)
+            pltpu.make_async_copy(slot.at[0, :, cols], wbuf.at[j], sem.at[j]).start()
+
+    for j in order:
+        pltpu.make_async_copy(wbuf.at[j], wbuf.at[j], sem.at[j]).wait()
+        y = nn_dot(h[...], wbuf[j])
+        for r in range(CAP):
+            part = y[128 * r : 128 * (r + 1)]
+            at = r if j < 3 else 6 + r // 3
+            left = PART * (j if j < 3 else r % 3)
+            for c in range(0, PART, 128):
+                tile = ROWS * ((left + c) // 128) + at
+                wide[pl.ds(tile, 128, stride=8), :] = part[:, c : c + 128]
+        if j < 3:
+            for c in range(4 * j, 4 * (j + 1)):
+                block = wide[ROWS * c : ROWS * (c + 1), :]
+                left = 128 * (c - 4 * j)
+                packed[j, :, left : left + 128] = block.astype(BF16)
+            target = out.at[:, pl.ds(PART * j, PART)]
+            sends.append(pltpu.make_async_copy(packed.at[j], target, sem_out.at[j]))
+            sends[-1].start()
+    for c in sends:
+        c.wait()
 
 
 def weigh_kernel(route, gate, out):
@@ -264,6 +277,10 @@
     out[:, WIDE:] = tail.astype(BF16)
 
 
+def hbm(x):
+    return pltpu.with_memory_space_constraint(x, pltpu.HBM)
+
+
 def resident(x):
     return pltpu.with_memory_space_constraint(x, pltpu.VMEM)
 
@@ -299,13 +316,13 @@
         held = [2] * (count > 1) + list(dims)
         return pl.pallas_call(
             stage_kernel,
-            out_shape=[shape(*held)] * 3,
-            in_specs=[SMEM] * 3 + [ANY] * count,
-            out_specs=[ANY] * 3,
+            out_shape=[pltpu.HBM(tuple(held), BF16)] * 3,
+            in_specs=[SMEM] * 3 + [HBM] * count,
+            out_specs=[HBM] * 3,
             scratch_shapes=[pltpu.VMEM((2, *dims), BF16)] * count
             + [pltpu.SemaphoreType.DMA((count,)), pltpu.SemaphoreType.DMA((3 * count,))],
             compiler_params=params(),
-        )(*where, *sources)
+        )(*where, *[hbm(v) for v in sources])
 
     swapped_up = swap(new_gate_up)
     swapped_down = swap(new_down)
@@ -338,7 +355,7 @@
         got_down.append(move(both[k - 1], k))
     weight = pl.pallas_call(
         weigh_kernel,
-        out_shape=shape(4, 2 * TOK, ROWS),
+        out_shape=pltpu.HBM((4, 2 * TOK, ROWS), BF16),
         in_specs=[VMEM, VMEM],
         out_specs=VMEM,
         compiler_params=params(),
@@ -346,7 +363,7 @@
     )(route, gate)
     rows = pl.pallas_call(
         compact_kernel,
-        out_shape=shape(DENSE, D),
+        out_shape=pltpu.VMEM((DENSE, D), BF16),
         in_specs=[VMEM],
         out_specs=VMEM,
         compiler_params=params(),
@@ -354,22 +371,28 @@
     )(incoming)
     hidden = pl.pallas_call(
         up_kernel,
-        out_shape=shape(DENSE, FF),
-        in_specs=[SMEM] * 3 + [VMEM] + [ANY] * 9,
+        out_shape=pltpu.VMEM((DENSE, FF), BF16),
+        in_specs=[SMEM] * 3 + [VMEM] + [HBM] * 9,
         out_specs=VMEM,
         scratch_shapes=[pltpu.VMEM((2, 2, D, 256), BF16), pltpu.SemaphoreType.DMA((2,))],
-        compiler_params=params(),
+        compiler_params=params(28),
         name="up",
-    )(*where, rows, new_gate_up, swapped_up, *got_up, slot_gate_up)
+    )(*where, resident(rows), *[hbm(v) for v in (new_gate_up, swapped_up, *got_up, slot_gate_up)])
     results = pl.pallas_call(
         down_kernel,
-        out_shape=shape(ROWS, WIDE),
-        in_specs=[SMEM] * 3 + [VMEM] + [ANY] * 6,
-        out_specs=VMEM,
-        scratch_shapes=[pltpu.VMEM((FF, D), BF16), pltpu.SemaphoreType.DMA((1,))],
-        compiler_params=params(),
+        out_shape=pltpu.HBM((ROWS, WIDE), BF16),
+        in_specs=[SMEM] * 3 + [VMEM] + [HBM] * 6,
+        out_specs=HBM,
+        scratch_shapes=[
+            pltpu.VMEM((4, FF, PART), BF16),
+            pltpu.VMEM((ROWS * WIDE // 128, 128), F32),
+            pltpu.VMEM((3, ROWS, PART), BF16),
+            pltpu.SemaphoreType.DMA((4,)),
+            pltpu.SemaphoreType.DMA((3,)),
+        ],
+        compiler_params=params(28),
         name="down",
-    )(*where, hidden, new_down, swapped_down, *got_down, slot_down)
+    )(*where, resident(hidden), *[hbm(v) for v in (new_down, swapped_down, *got_down, slot_down)])
     returned = lax.all_to_all(
         results.reshape(SLOTS, PACK, WIDE), EVERY, split_axis=0, concat_axis=0, tiled=True
     )
@@ -381,7 +404,7 @@
         out_specs=VMEM,
         compiler_params=params(),
         name="combine",
-    )(weight, returned)
+    )(hbm(weight), returned)
 
 
 def solution(mesh):

time: 240 us -> 239 us (level)
  Pallas kernels: 43.2 us -> 34.6 us
  waiting for transfers between devices: 135 us -> 141 us
    pallas_call x7, Pallas kernels: 35.3 us -> 28.4 us  [the longest x3 10.3 us: stage(): pl.pallas_call(stage_kernel, out_shape=[pltpu.HBM(tuple(held), BF16)] * 3...]
    ppermute x9, waiting for transfers between devices: 47.7 us -> 52 us  [move(): return lax.ppermute(x, DP, [(d ^ k, d) for d in range(ACTIVE)])]
  transfers between devices with their start and end apart: 16 -> 16, of which waited for: 8 -> 8; matrix products, arithmetic and copies ran while one was open for 0% -> 0% of each run, Pallas kernels for 13% -> 10%
where the time goes in v1:
time: 239 us; the launch traced here: 238 us
  waiting for transfers between devices  141 us (59%)
  starting transfers between devices  56.6 us (24%)
  Pallas kernels  34.6 us (14%)
  local copies, waits for them, and re-layouts  3.52 us (1%)
    ppermute x9, waiting for transfers between devices, move(): return lax.ppermute(x, DP, [(d ^ k, d) for d in range(ACTIVE)])  52 us
    all_to_all x1, waiting for transfers between devices, per_device(): lax.all_to_all(results.reshape(SLOTS, PACK, WIDE), EVERY, split_axis=0, c...  39.7 us
    ppermute x2, waiting for transfers between devices, swap(): return lax.ppermute(x, 'zl', [(0, 1), (1, 0)])  37.1 us
    ppermute x9, starting transfers between devices, move(): return lax.ppermute(x, DP, [(d ^ k, d) for d in range(ACTIVE)])  26.8 us
    ppermute x3, waiting for transfers between devices, per_device(): packed.append(lax.ppermute(packed[0], 'x', [(d ^ k, d) for d in range(4)]))  12.2 us
    all_to_all x1, starting transfers between devices, per_device(): lax.all_to_all(results.reshape(SLOTS, PACK, WIDE), EVERY, split_axis=0, c...  11.6 us
    all_to_all x1, starting transfers between devices, per_device(): lax.all_to_all(outgoing.reshape(32, 4 * PACK, WIDE), COLUMN, split_axis=0...  10.3 us
    pallas_call x3, Pallas kernels, stage(): pl.pallas_call(stage_kernel, out_shape=[pltpu.HBM(tuple(held), BF16)] * 3...  10.3 us
  transfers between devices with their start and end apart: 16, of which 8 were waited for; matrix products, arithmetic and copies ran while one was open for 0% of the time, Pallas kernels for 10%

profile of v1, /device:TPU:1, one launch (start us, length us, event | category | flops | bytes accessed | tf_op | source)
XLA Modules:
  0.0 237.8 jit_solution(2645784380441869894)
XLA Ops:
  1.8 2.1 collective-permute-start
  3.9 2.5 %collective-permute-start.1 = (bf16[64,2176]{1,0:T(8,128)(2,1)S(1)}, bf16[64,2176]{1,0:T(8,128)(2,1)S(1)}, u32[]{:S(2)}, u32[]{:S(2)}) collective-permute-start(bf16[64,2176]{1,0:T(8,128)(2,1)S(1)} %fusion.1.refs_0_), channel_id=1, source_target_pairs={{2,0},{3,1},{0,2},{1,3},{6,4},{7,5},{4,6},{5,7},{10,8},{11,9},{8,1... | collective-permute-start | bytes 835592 | tf_op jit(solution)/shard_map/ppermute | solution.py:332
  6.4 1.8 collective-permute-start.3
  8.2 1.6 collective-permute-done.refs_1_
  9.8 8.6 %collective-permute-done.1.refs_2_ = bf16[64,2176]{1,0:T(8,128)(2,1)S(1)} collective-permute-done((bf16[64,2176]{1,0:T(8,128)(2,1)S(1)}, bf16[64,2176]{1,0:T(8,128)(2,1)S(1)}, u32[]{:S(2)}, u32[]{:S(2)}) %collective-permute-start.1) | collective-permute-done | bytes 278560 | tf_op jit(solution)/shard_map/ppermute | solution.py:332
  18.4 2.1 collective-permute-done.2.refs_3_
  20.5 3.3 %dispatch.1 = bf16[32,4,8,1536]{3,2,1,0:T(8,128)(2,1)S(1)} custom-call(s32[2]{0:T(128)S(1)} %pad_add_fusion.ids, bf16[64,2176]{1,0:T(8,128)(2,1)S(1)} %fusion.1.refs_0_, bf16[64,2176]{1,0:T(8,128)(2,1)S(1)} %collective-permute-done.refs_1_, bf16[64,2176]{1,0:T(8,128)(2,1)S(1)} %collective-permute-done.1.refs_2_, ...), custom_call_target="tpu_custom_call" | custom-call | tf_op jit(solution)/shard_map/dispatch/pallas_call | solution.py:337
  23.8 1.6 copy-done
  25.4 10.3 %all-to-all-start = ((bf16[32,32,1536]{2,1,0:T(8,128)(2,1)}), bf16[32,32,1536]{2,1,0:T(8,128)(2,1)S(1)}, u32[]{:S(2)}, u32[]{:S(2)}) async-start(bf16[32,32,1536]{2,1,0:T(8,128)(2,1)} %bitcast.9), calls=%async_computation | async-start | bytes 6291456 | tf_op jit(solution)/shard_map/all_to_all | solution.py:345
  35.7 1.4 collective-permute-start.10
  37.2 3.4 %shard_map.91 = (bf16[256,1536]{1,0:T(8,128)(2,1)}, bf16[256,1536]{1,0:T(8,128)(2,1)}, bf16[256,1536]{1,0:T(8,128)(2,1)}) custom-call(s32[2]{0:T(128)S(1)} %pad_add_fusion.ids, s32[128]{0:T(128)S(1)} %copy-done.2, s32[32]{0:T(128)S(1)} %copy-done.3, bf16[2,256,1536]{2,1,0:T(8,128)(2,1)} %own.2), custom_call_target="tpu_custom_call" | custom-call | tf_op jit(solution)/shard_map/pallas_call | solution.py:317
  40.6 1.9 collective-permute-start.4
  42.5 3.3 %collective-permute-start.5 = (bf16[256,1536]{1,0:T(8,128)(2,1)}, bf16[256,1536]{1,0:T(8,128)(2,1)S(1)}, u32[]{:S(2)}, u32[]{:S(2)}) collective-permute-start(bf16[256,1536]{1,0:T(8,128)(2,1)} %get-tuple-element.15), channel_id=1, source_target_pairs={{2,0},{3,1},{0,2},{1,3},{6,4},{7,5},{10,8},{11,9},{8,10},{9,11},{1... | collective-permute-start | bytes 2359304 | tf_op jit(solution)/shard_map/ppermute | solution.py:312
  45.8 4.4 %collective-permute-start.6 = (bf16[256,1536]{1,0:T(8,128)(2,1)}, bf16[256,1536]{1,0:T(8,128)(2,1)S(1)}, u32[]{:S(2)}, u32[]{:S(2)}) collective-permute-start(bf16[256,1536]{1,0:T(8,128)(2,1)} %get-tuple-element.16), channel_id=1, source_target_pairs={{3,0},{2,1},{1,2},{0,3},{7,4},{6,5},{11,8},{10,9},{9,10},{8,11},{1... | collective-permute-start | bytes 2359304 | tf_op jit(solution)/shard_map/ppermute | solution.py:312
  50.2 3.4 %shard_map.92 = (bf16[256,1536]{1,0:T(8,128)(2,1)}, bf16[256,1536]{1,0:T(8,128)(2,1)}, bf16[256,1536]{1,0:T(8,128)(2,1)}) custom-call(s32[2]{0:T(128)S(1)} %pad_add_fusion.ids, s32[128]{0:T(128)S(1)} %copy-done.2, s32[32]{0:T(128)S(1)} %copy-done.3, bf16[2,256,1536]{2,1,0:T(8,128)(2,1)} %collective-permute-done.3.refs_0_.swapped), custom_call_target="tpu_custom_call" | custom-call | tf_op jit(solution)/shard_map/pallas_call | solution.py:317
  53.7 1.9 collective-permute-start.7
  55.6 37.1 %collective-permute-done.10.refs_1_.swapped = bf16[2,96,2048]{2,1,0:T(8,128)(2,1)S(1)} collective-permute-done((bf16[2,96,2048]{2,1,0:T(8,128)(2,1)}, bf16[2,96,2048]{2,1,0:T(8,128)(2,1)S(1)}, u32[]{:S(2)}, u32[]{:S(2)}) %collective-permute-start.10) | collective-permute-done | bytes 786464 | tf_op jit(solution)/shard_map/ppermute | solution.py:309
  93.6 3.5 %shard_map.93 = (bf16[2,96,2048]{2,1,0:T(8,128)(2,1)}, bf16[2,96,2048]{2,1,0:T(8,128)(2,1)}, bf16[2,96,2048]{2,1,0:T(8,128)(2,1)}) custom-call(s32[2]{0:T(128)S(1)} %pad_add_fusion.ids, s32[128]{0:T(128)S(1)} %copy-done.2, s32[32]{0:T(128)S(1)} %copy-done.3, bf16[2,96,2048]{2,1,0:T(8,128)(2,1)} %own.3, bf16[2,96,2048]{2,1,0:T(8,128)(2,1)} %copy-done.5), custom_call_target="tpu_custom_call" | custom-call | tf_op jit(solution)/shard_map/pallas_call | solution.py:317
  97.1 1.9 collective-permute-start.11
  99.0 5.0 %collective-permute-start.8 = (bf16[256,1536]{1,0:T(8,128)(2,1)}, bf16[256,1536]{1,0:T(8,128)(2,1)}, u32[]{:S(2)}, u32[]{:S(2)}) collective-permute-start(bf16[256,1536]{1,0:T(8,128)(2,1)} %get-tuple-element.18), channel_id=1, source_target_pairs={{2,0},{3,1},{0,2},{1,3},{6,4},{7,5},{10,8},{11,9},{8,10},{9,11},{1... | collective-permute-start | bytes 2359304 | tf_op jit(solution)/shard_map/ppermute | solution.py:312
  104.0 2.7 %collective-permute-start.9 = (bf16[256,1536]{1,0:T(8,128)(2,1)}, bf16[256,1536]{1,0:T(8,128)(2,1)}, u32[]{:S(2)}, u32[]{:S(2)}) collective-permute-start(bf16[256,1536]{1,0:T(8,128)(2,1)} %get-tuple-element.19), channel_id=1, source_target_pairs={{3,0},{2,1},{1,2},{0,3},{7,4},{6,5},{11,8},{10,9},{9,10},{8,11},{1... | collective-permute-start | bytes 2359304 | tf_op jit(solution)/shard_map/ppermute | solution.py:312
  106.7 2.3 collective-permute-start.12
  110.0 3.4 %collective-permute-start.13 = (bf16[2,96,2048]{2,1,0:T(8,128)(2,1)}, bf16[2,96,2048]{2,1,0:T(8,128)(2,1)}, u32[]{:S(2)}, u32[]{:S(2)}) collective-permute-start(bf16[2,96,2048]{2,1,0:T(8,128)(2,1)} %get-tuple-element.22), channel_id=1, source_target_pairs={{3,0},{2,1},{1,2},{0,3},{7,4},{6,5},{11,8},{10,9},{9,10},{8,11},{1... | collective-permute-start | bytes 2359304 | tf_op jit(solution)/shard_map/ppermute | solution.py:312
  114.7 20.0 %collective-permute-done.8.refs_4_ = bf16[256,1536]{1,0:T(8,128)(2,1)} collective-permute-done((bf16[256,1536]{1,0:T(8,128)(2,1)}, bf16[256,1536]{1,0:T(8,128)(2,1)}, u32[]{:S(2)}, u32[]{:S(2)}) %collective-permute-start.8) | collective-permute-done | bytes 786464 | tf_op jit(solution)/shard_map/ppermute | solution.py:312
  134.7 22.8 %collective-permute-done.9.refs_5_ = bf16[256,1536]{1,0:T(8,128)(2,1)} collective-permute-done((bf16[256,1536]{1,0:T(8,128)(2,1)}, bf16[256,1536]{1,0:T(8,128)(2,1)}, u32[]{:S(2)}, u32[]{:S(2)}) %collective-permute-start.9) | collective-permute-done | bytes 786464 | tf_op jit(solution)/shard_map/ppermute | solution.py:312
  157.5 7.6 %up.1.h = bf16[768,768]{1,0:T(8,128)(2,1)S(1)} custom-call(s32[2]{0:T(128)S(1)} %pad_add_fusion.ids, s32[128]{0:T(128)S(1)} %copy-done.2, s32[32]{0:T(128)S(1)} %copy-done.3, bf16[768,2048]{1,0:T(8,128)(2,1)S(1)} %compact.1.x, bf16[2,256,1536]{2,1,0:T(8,128)(2,1)} %own.2, bf16[2,256,1536]{2,1,0:T(8,128)(2,1)} %collective-permute-done.3.refs_0_.swapped, ...), custom_call_target="tpu_custom_call" | custom-call | tf_op jit(solution)/shard_map/up/pallas_call | solution.py:372
  165.2 9.2 %collective-permute-done.13.refs_2_ = bf16[2,96,2048]{2,1,0:T(8,128)(2,1)} collective-permute-done((bf16[2,96,2048]{2,1,0:T(8,128)(2,1)}, bf16[2,96,2048]{2,1,0:T(8,128)(2,1)}, u32[]{:S(2)}, u32[]{:S(2)}) %collective-permute-start.13) | collective-permute-done | bytes 786464 | tf_op jit(solution)/shard_map/ppermute | solution.py:312
  174.3 7.2 %down.1 = bf16[1024,1536]{1,0:T(8,128)(2,1)} custom-call(s32[2]{0:T(128)S(1)} %pad_add_fusion.ids, s32[128]{0:T(128)S(1)} %copy-done.2, s32[32]{0:T(128)S(1)} %copy-done.3, bf16[768,768]{1,0:T(8,128)(2,1)S(1)} %up.1.h, bf16[2,96,2048]{2,1,0:T(8,128)(2,1)} %own.3, bf16[2,96,2048]{2,1,0:T(8,128)(2,1)} %copy-done.5, ...), custom_call_target="tpu_custom_call" | custom-call | tf_op jit(solution)/shard_map/down/pallas_call | solution.py:381
  181.6 11.6 %all-to-all-start.1 = ((bf16[128,8,1536]{2,1,0:T(8,128)(2,1)}), bf16[128,8,1536]{2,1,0:T(8,128)(2,1)S(1)}, u32[]{:S(2)}, u32[]{:S(2)}) async-start(bf16[128,8,1536]{2,1,0:T(8,128)(2,1)} %bitcast.13), calls=%async_computation.1 | async-start | bytes 6291456 | tf_op jit(solution)/shard_map/all_to_all | solution.py:396
  193.3 1.9 weigh.1.weight
  195.2 39.7 %all-to-all-done.1 = bf16[128,8,1536]{2,1,0:T(8,128)(2,1)S(1)} async-done(((bf16[128,8,1536]{2,1,0:T(8,128)(2,1)}), bf16[128,8,1536]{2,1,0:T(8,128)(2,1)S(1)}, u32[]{:S(2)}, u32[]{:S(2)}) %all-to-all-start.1) | async-done | bytes 3145760 | tf_op jit(solution)/shard_map/all_to_all | solution.py:396
  234.9 2.9 %combine.1 = bf16[64,2048]{1,0:T(8,128)(2,1)} custom-call(bf16[4,128,1024]{2,1,0:T(8,128)(2,1)} %weigh.1.weight, bf16[1024,1536]{1,0:T(8,128)(2,1)S(1)} %bitcast.10), custom_call_target="tpu_custom_call" | custom-call | tf_op jit(solution)/shard_map/combine/pallas_call | solution.py:400
  (33 shorter events, 5.0 us)
Async XLA Ops:
  1.8 8.1 %collective-permute-start = (bf16[64,2176]{1,0:T(8,128)(2,1)S(1)}, bf16[64,2176]{1,0:T(8,128)(2,1)S(1)}, u32[]{:S(2)}, u32[]{:S(2)}) collective-permute-start(bf16[64,2176]{1,0:T(8,128)(2,1)S(1)} %fusion.1.refs_0_), channel_id=1, source_target_pairs={{1,0},{0,1},{3,2},{2,3},{5,4},{4,5},{7,6},{6,7},{9,8},{8,9},{11,10... | collective-permute-start | bytes 835592 | tf_op jit(solution)/shard_map/ppermute | solution.py:332
  3.9 14.5 %collective-permute-start.1 = (bf16[64,2176]{1,0:T(8,128)(2,1)S(1)}, bf16[64,2176]{1,0:T(8,128)(2,1)S(1)}, u32[]{:S(2)}, u32[]{:S(2)}) collective-permute-start(bf16[64,2176]{1,0:T(8,128)(2,1)S(1)} %fusion.1.refs_0_), channel_id=1, source_target_pairs={{2,0},{3,1},{0,2},{1,3},{6,4},{7,5},{4,6},{5,7},{10,8},{11,9},{8,1... | collective-permute-start | bytes 835592 | tf_op jit(solution)/shard_map/ppermute | solution.py:332
  6.3 14.2 %collective-permute-start.2 = (bf16[64,2176]{1,0:T(8,128)(2,1)S(1)}, bf16[64,2176]{1,0:T(8,128)(2,1)S(1)}, u32[]{:S(2)}, u32[]{:S(2)}) collective-permute-start(bf16[64,2176]{1,0:T(8,128)(2,1)S(1)} %fusion.1.refs_0_), channel_id=1, source_target_pairs={{3,0},{2,1},{1,2},{0,3},{7,4},{6,5},{5,6},{4,7},{11,8},{10,9},{9,1... | collective-permute-start | bytes 835592 | tf_op jit(solution)/shard_map/ppermute | solution.py:332
  6.4 43.9 %collective-permute-start.3 = (bf16[2,256,1536]{2,1,0:T(8,128)(2,1)}, bf16[2,256,1536]{2,1,0:T(8,128)(2,1)}, u32[]{:S(2)}, u32[]{:S(2)}) collective-permute-start(bf16[2,256,1536]{2,1,0:T(8,128)(2,1)} %own.2), channel_id=1, source_target_pairs={{0,4},{4,0},{1,5},{5,1},{2,6},{6,2},{3,7},{7,3},{8,12},{12,8},{9,1... | collective-permute-start | bytes 4718600 | tf_op jit(solution)/shard_map/ppermute | solution.py:309
  23.8 1.6 copy-start
  25.4 11.8 %copy-start.2 = (s32[128]{0:T(128)S(1)}, s32[128]{0:T(128)}, u32[]{:S(2)}) copy-start(s32[128]{0:T(128)} %table.9) | copy-start | bytes 1540
  25.4 11.8 %copy-start.3 = (s32[32]{0:T(128)S(1)}, s32[32]{0:T(128)}, u32[]{:S(2)}) copy-start(s32[32]{0:T(128)} %refreshed.9) | copy-start | bytes 388
  25.4 88.0 %all-to-all-start = ((bf16[32,32,1536]{2,1,0:T(8,128)(2,1)}), bf16[32,32,1536]{2,1,0:T(8,128)(2,1)S(1)}, u32[]{:S(2)}, u32[]{:S(2)}) async-start(bf16[32,32,1536]{2,1,0:T(8,128)(2,1)} %bitcast.9), calls=%async_computation | async-start | bytes 6291456 | tf_op jit(solution)/shard_map/all_to_all | solution.py:345
  35.7 57.0 %collective-permute-start.10 = (bf16[2,96,2048]{2,1,0:T(8,128)(2,1)}, bf16[2,96,2048]{2,1,0:T(8,128)(2,1)S(1)}, u32[]{:S(2)}, u32[]{:S(2)}) collective-permute-start(bf16[2,96,2048]{2,1,0:T(8,128)(2,1)} %own.3), channel_id=1, source_target_pairs={{0,4},{4,0},{1,5},{5,1},{2,6},{6,2},{3,7},{7,3},{8,12},{12,8},{9,1... | collective-permute-start | bytes 2359304 | tf_op jit(solution)/shard_map/ppermute | solution.py:309
  40.6 58.4 %collective-permute-start.4 = (bf16[256,1536]{1,0:T(8,128)(2,1)}, bf16[256,1536]{1,0:T(8,128)(2,1)S(1)}, u32[]{:S(2)}, u32[]{:S(2)}) collective-permute-start(bf16[256,1536]{1,0:T(8,128)(2,1)} %get-tuple-element.14), channel_id=1, source_target_pairs={{1,0},{0,1},{3,2},{2,3},{5,4},{4,5},{9,8},{8,9},{11,10},{10,11},{1... | collective-permute-start | bytes 2359304 | tf_op jit(solution)/shard_map/ppermute | solution.py:312
  42.5 61.5 %collective-permute-start.5 = (bf16[256,1536]{1,0:T(8,128)(2,1)}, bf16[256,1536]{1,0:T(8,128)(2,1)S(1)}, u32[]{:S(2)}, u32[]{:S(2)}) collective-permute-start(bf16[256,1536]{1,0:T(8,128)(2,1)} %get-tuple-element.15), channel_id=1, source_target_pairs={{2,0},{3,1},{0,2},{1,3},{6,4},{7,5},{10,8},{11,9},{8,10},{9,11},{1... | collective-permute-start | bytes 2359304 | tf_op jit(solution)/shard_map/ppermute | solution.py:312
  45.8 60.9 %collective-permute-start.6 = (bf16[256,1536]{1,0:T(8,128)(2,1)}, bf16[256,1536]{1,0:T(8,128)(2,1)S(1)}, u32[]{:S(2)}, u32[]{:S(2)}) collective-permute-start(bf16[256,1536]{1,0:T(8,128)(2,1)} %get-tuple-element.16), channel_id=1, source_target_pairs={{3,0},{2,1},{1,2},{0,3},{7,4},{6,5},{11,8},{10,9},{9,10},{8,11},{1... | collective-permute-start | bytes 2359304 | tf_op jit(solution)/shard_map/ppermute | solution.py:312
  53.7 55.4 %collective-permute-start.7 = (bf16[256,1536]{1,0:T(8,128)(2,1)}, bf16[256,1536]{1,0:T(8,128)(2,1)S(1)}, u32[]{:S(2)}, u32[]{:S(2)}) collective-permute-start(bf16[256,1536]{1,0:T(8,128)(2,1)} %get-tuple-element.17), channel_id=1, source_target_pairs={{1,0},{0,1},{3,2},{2,3},{5,4},{4,5},{9,8},{8,9},{11,10},{10,11},{1... | collective-permute-start | bytes 2359304 | tf_op jit(solution)/shard_map/ppermute | solution.py:312
  92.7 0.9 copy-start.5
  97.1 68.1 %collective-permute-start.11 = (bf16[2,96,2048]{2,1,0:T(8,128)(2,1)}, bf16[2,96,2048]{2,1,0:T(8,128)(2,1)}, u32[]{:S(2)}, u32[]{:S(2)}) collective-permute-start(bf16[2,96,2048]{2,1,0:T(8,128)(2,1)} %get-tuple-element.20), channel_id=1, source_target_pairs={{1,0},{0,1},{3,2},{2,3},{5,4},{4,5},{9,8},{8,9},{11,10},{10,11},{1... | collective-permute-start | bytes 2359304 | tf_op jit(solution)/shard_map/ppermute | solution.py:312
  99.0 10.1 %copy-start.6 = (bf16[256,1536]{1,0:T(8,128)(2,1)}, bf16[256,1536]{1,0:T(8,128)(2,1)S(1)}, u32[]{:S(2)}) copy-start(bf16[256,1536]{1,0:T(8,128)(2,1)S(1)} %collective-permute-done.4.refs_0_) | copy-start | bytes 2359300
  99.0 35.7 %collective-permute-start.8 = (bf16[256,1536]{1,0:T(8,128)(2,1)}, bf16[256,1536]{1,0:T(8,128)(2,1)}, u32[]{:S(2)}, u32[]{:S(2)}) collective-permute-start(bf16[256,1536]{1,0:T(8,128)(2,1)} %get-tuple-element.18), channel_id=1, source_target_pairs={{2,0},{3,1},{0,2},{1,3},{6,4},{7,5},{10,8},{11,9},{8,10},{9,11},{1... | collective-permute-start | bytes 2359304 | tf_op jit(solution)/shard_map/ppermute | solution.py:312
  104.0 5.1 %copy-start.7 = (bf16[256,1536]{1,0:T(8,128)(2,1)}, bf16[256,1536]{1,0:T(8,128)(2,1)S(1)}, u32[]{:S(2)}) copy-start(bf16[256,1536]{1,0:T(8,128)(2,1)S(1)} %collective-permute-done.5.refs_1_) | copy-start | bytes 2359300
  104.0 53.5 %collective-permute-start.9 = (bf16[256,1536]{1,0:T(8,128)(2,1)}, bf16[256,1536]{1,0:T(8,128)(2,1)}, u32[]{:S(2)}, u32[]{:S(2)}) collective-permute-start(bf16[256,1536]{1,0:T(8,128)(2,1)} %get-tuple-element.19), channel_id=1, source_target_pairs={{3,0},{2,1},{1,2},{0,3},{7,4},{6,5},{11,8},{10,9},{9,10},{8,11},{1... | collective-permute-start | bytes 2359304 | tf_op jit(solution)/shard_map/ppermute | solution.py:312
  106.7 2.4 %copy-start.8 = (bf16[256,1536]{1,0:T(8,128)(2,1)}, bf16[256,1536]{1,0:T(8,128)(2,1)S(1)}, u32[]{:S(2)}) copy-start(bf16[256,1536]{1,0:T(8,128)(2,1)S(1)} %collective-permute-done.6.refs_2_) | copy-start | bytes 2359300
  106.7 58.4 %collective-permute-start.12 = (bf16[2,96,2048]{2,1,0:T(8,128)(2,1)}, bf16[2,96,2048]{2,1,0:T(8,128)(2,1)}, u32[]{:S(2)}, u32[]{:S(2)}) collective-permute-start(bf16[2,96,2048]{2,1,0:T(8,128)(2,1)} %get-tuple-element.21), channel_id=1, source_target_pairs={{2,0},{3,1},{0,2},{1,3},{6,4},{7,5},{10,8},{11,9},{8,10},{9,11},{1... | collective-permute-start | bytes 2359304 | tf_op jit(solution)/shard_map/ppermute | solution.py:312
  109.1 0.9 copy-start.9
  110.0 64.4 %collective-permute-start.13 = (bf16[2,96,2048]{2,1,0:T(8,128)(2,1)}, bf16[2,96,2048]{2,1,0:T(8,128)(2,1)}, u32[]{:S(2)}, u32[]{:S(2)}) collective-permute-start(bf16[2,96,2048]{2,1,0:T(8,128)(2,1)} %get-tuple-element.22), channel_id=1, source_target_pairs={{3,0},{2,1},{1,2},{0,3},{7,4},{6,5},{11,8},{10,9},{9,10},{8,11},{1... | collective-permute-start | bytes 2359304 | tf_op jit(solution)/shard_map/ppermute | solution.py:312
  181.6 11.7 %copy-start.1 = (s32[64,8]{0,1:T(8,128)S(1)}, s32[64,8]{0,1:T(8,128)}, u32[]{:S(2)}) copy-start(s32[64,8]{0,1:T(8,128)} %param.10) | copy-start | bytes 6148
  181.6 11.7 %copy-start.4 = (f32[64,8]{0,1:T(8,128)S(1)}, f32[64,8]{0,1:T(8,128)}, u32[]{:S(2)}) copy-start(f32[64,8]{0,1:T(8,128)} %param.11) | copy-start | bytes 6148
  181.6 53.3 %all-to-all-start.1 = ((bf16[128,8,1536]{2,1,0:T(8,128)(2,1)}), bf16[128,8,1536]{2,1,0:T(8,128)(2,1)S(1)}, u32[]{:S(2)}, u32[]{:S(2)}) async-start(bf16[128,8,1536]{2,1,0:T(8,128)(2,1)} %bitcast.13), calls=%async_computation.1 | async-start | bytes 6291456 | tf_op jit(solution)/shard_map/all_to_all | solution.py:396

commit v2 on v1

--- a/solution.py
+++ b/solution.py
@@ -89,6 +89,10 @@
 
 
 def stage_kernel(ids, table, refreshed, *refs):
+    if len(refs) == 5:
+        picks = [pick_of(ids, table, refreshed, ids[1] ^ k) for k in range(1, 4)]
+        copy_all([(refs[0].at[picks[k]], refs[1 + k]) for k in range(3)], refs[4])
+        return
     count = (len(refs) - 5) // 2
     sources, outs, sem_in, sem_out = refs[:count], refs[count : count + 3], refs[-2], refs[-1]
     held = refs[count + 3 : -2]
@@ -105,28 +109,22 @@
 
 
 def dispatch_kernel(ids, *refs):
-    packed, out = refs[:4], refs[4]
+    routes, near, out = refs[:4], refs[4:8], refs[8]
     column = ids[1] & 3
-    lanes = iota((TOK, SLOTS), 1)
-    lower = (iota((TOK, TOK), 0) > iota((TOK, TOK), 1)).astype(F32).astype(BF16)
     part = 32 * PACK
     every = (iota((part, SLOTS), 1) == 4 * (iota((part, SLOTS), 0) >> 3) + column).astype(F32)
     every = every.astype(BF16)
     place = (iota((part, SLOTS), 0) & 7).astype(F32)
     left = iota((part, SLOTS), 1) < TOK
     for k in range(4):
-        home = home_of(packed[k][:, D:].astype(F32).astype(jnp.int32))
-        hits = jnp.zeros((TOK, SLOTS), F32)
-        for n in range(TOP):
-            hits = jnp.where(home[:, n : n + 1] == lanes, 1.0, hits)
-        rank = jnp.where(hits > 0, nn_dot(lower, hits.astype(BF16)), -1.0).astype(BF16)
-        wide = nt_dot(every, jnp.concatenate([rank, rank], axis=0))
+        rank = ranks(home_of(routes[k][...]))
+        wide = nn_dot(every, jnp.concatenate([rank, rank], axis=1))
         main = left & (wide == place) & (place < CAP)
         for j in range(3):
             wanted = jnp.where(place == 6, float(j), jnp.where(place == 7, float(3 + j), -2.0))
             pick = (main | (jnp.logical_not(left) & (wide == wanted))).astype(F32).astype(BF16)
             cols = slice(PART * j, PART * (j + 1))
-            rhs = jnp.concatenate([packed[k][:, cols], packed[k][:, WIDE:D]], axis=0)
+            rhs = jnp.concatenate([near[k][:, cols], near[k][:, WIDE:]], axis=0)
             got = nn_dot(pick, rhs).reshape(32, PACK, PART)
             out[:, column ^ k, :, cols] = got.astype(BF16)
 
@@ -311,6 +309,16 @@
     def move(x, k):
         return lax.ppermute(x, DP, [(d ^ k, d) for d in range(ACTIVE)])
 
+    def stage_held(dims, source):
+        return pl.pallas_call(
+            stage_kernel,
+            out_shape=[pltpu.HBM(dims, BF16)] * 3,
+            in_specs=[SMEM] * 3 + [VMEM],
+            out_specs=[HBM] * 3,
+            scratch_shapes=[pltpu.SemaphoreType.DMA((3,))],
+            compiler_params=params(),
+        )(*where, resident(source))
+
     def stage(dims, *sources):
         count = len(sources)
         held = [2] * (count > 1) + list(dims)
@@ -326,10 +334,12 @@
 
     swapped_up = swap(new_gate_up)
     swapped_down = swap(new_down)
-    marks = jnp.pad(slot_route.astype(BF16), ((0, 0), (0, 120)))
-    packed = [jnp.concatenate([tokens, marks], axis=1)]
+    near = [tokens]
+    routes = [route]
     for k in range(1, 4):
-        packed.append(lax.ppermute(packed[0], "x", [(d ^ k, d) for d in range(4)]))
+        pairs = [(d ^ k, d) for d in range(4)]
+        near.append(lax.ppermute(tokens, "x", pairs))
+        routes.append(lax.ppermute(route, "x", pairs))
     own = stage((256, WIDE), new_gate_up)
     got_up = []
     for k in range(1, 4):
@@ -337,16 +347,16 @@
     outgoing = pl.pallas_call(
         dispatch_kernel,
         out_shape=shape(32, 4, PACK, WIDE),
-        in_specs=[SMEM] + [VMEM] * 4,
+        in_specs=[SMEM] + [VMEM] * 8,
         out_specs=VMEM,
         compiler_params=params(),
         name="dispatch",
-    )(ids, *[resident(p) for p in packed])
+    )(ids, *routes, *[resident(p) for p in near])
     incoming = lax.all_to_all(
         outgoing.reshape(32, 4 * PACK, WIDE), COLUMN, split_axis=0, concat_axis=0, tiled=True
     )
     incoming = resident(incoming.reshape(ROWS, WIDE))
-    far = stage((256, WIDE), swapped_up)
+    far = stage_held((256, WIDE), swapped_up)
     for k in range(1, 4):
         got_up.append(move(far[k - 1], k))
     both = stage((96, D), new_down, swapped_down)

time: 239 us -> 247 us (1.033)
  starting transfers between devices: 56.6 us -> 63.8 us
    ppermute x2, waiting for transfers between devices: 37.1 us -> 47 us  [swap(): return lax.ppermute(x, 'zl', [(0, 1), (1, 0)])]
    ppermute x3 -> x6, waiting for transfers between devices: 12.2 us -> 5.4 us  [the longest x3 5.39 us: per_device(): routes.append(lax.ppermute(route, 'x', pairs))]
    ppermute x3 -> x6, starting transfers between devices: 4.59 us -> 11.2 us  [the longest x3 6.73 us: per_device(): routes.append(lax.ppermute(route, 'x', pairs))]
    pallas_call x3 -> x2, Pallas kernels: 10.3 us -> 6.84 us  [stage(): pl.pallas_call(stage_kernel, out_shape=[pltpu.HBM(tuple(held), BF16)] * 3...]
    pallas_call x0 -> x1, Pallas kernels: none -> 2.86 us  [stage_held(): pl.pallas_call(stage_kernel, out_shape=[pltpu.HBM(dims, BF16)] * 3, in_sp...]
  transfers between devices with their start and end apart: 16 -> 19, of which waited for: 8 -> 8; matrix products, arithmetic and copies ran while one was open for 0% -> 0% of each run, Pallas kernels for 10% -> 10%
where the time goes in v2:
time: 247 us; the launch traced here: 246 us
  waiting for transfers between devices  143 us (58%)
  starting transfers between devices  63.8 us (26%)
  Pallas kernels  35.7 us (14%)
  local copies, waits for them, and re-layouts  3.44 us (1%)
    ppermute x9, waiting for transfers between devices, move(): return lax.ppermute(x, DP, [(d ^ k, d) for d in range(ACTIVE)])  50.9 us
    ppermute x2, waiting for transfers between devices, swap(): return lax.ppermute(x, 'zl', [(0, 1), (1, 0)])  47 us
    all_to_all x1, waiting for transfers between devices, per_device(): lax.all_to_all(results.reshape(SLOTS, PACK, WIDE), EVERY, split_axis=0, c...  39.6 us
    ppermute x9, starting transfers between devices, move(): return lax.ppermute(x, DP, [(d ^ k, d) for d in range(ACTIVE)])  26.1 us
    all_to_all x1, starting transfers between devices, per_device(): lax.all_to_all(results.reshape(SLOTS, PACK, WIDE), EVERY, split_axis=0, c...  13 us
    all_to_all x1, starting transfers between devices, per_device(): lax.all_to_all(outgoing.reshape(32, 4 * PACK, WIDE), COLUMN, split_axis=0...  10.5 us
    pallas_call x1, Pallas kernels, per_device(): pl.pallas_call(up_kernel, out_shape=pltpu.VMEM((DENSE, FF), BF16), in_spe...  7.63 us
    pallas_call x1, Pallas kernels, per_device(): pl.pallas_call(down_kernel, out_shape=pltpu.HBM((ROWS, WIDE), BF16), in_s...  7.16 us
  transfers between devices with their start and end apart: 19, of which 8 were waited for; matrix products, arithmetic and copies ran while one was open for 0% of the time, Pallas kernels for 10%

profile of v2, /device:TPU:1, one launch (start us, length us, event | category | flops | bytes accessed | tf_op | source)
XLA Modules:
  0.0 246.2 jit_solution(9937965048574627060)
XLA Ops:
  0.0 2.0 collective-permute-start.3
  2.0 2.5 collective-permute-start.4
  4.7 3.7 %collective-permute-start.1 = (s32[8,64]{1,0:T(8,128)}, s32[8,64]{1,0:T(8,128)S(1)}, u32[]{:S(2)}, u32[]{:S(2)}) collective-permute-start(s32[8,64]{1,0:T(8,128)} %bitcast.11), channel_id=1, source_target_pairs={{2,0},{3,1},{0,2},{1,3},{6,4},{7,5},{4,6},{5,7},{10,8},{11,9},{8,1... | collective-permute-start | bytes 6152 | tf_op jit(solution)/shard_map/ppermute | solution.py:342
  8.3 5.2 %collective-permute-done.refs_1_ = s32[8,64]{1,0:T(8,128)S(1)} collective-permute-done((s32[8,64]{1,0:T(8,128)}, s32[8,64]{1,0:T(8,128)S(1)}, u32[]{:S(2)}, u32[]{:S(2)}) %collective-permute-start) | collective-permute-done | bytes 2080 | tf_op jit(solution)/shard_map/ppermute | solution.py:342
  13.6 2.9 %collective-permute-start.2 = (s32[8,64]{1,0:T(8,128)}, s32[8,64]{1,0:T(8,128)S(1)}, u32[]{:S(2)}, u32[]{:S(2)}) collective-permute-start(s32[8,64]{1,0:T(8,128)} %bitcast.12), channel_id=1, source_target_pairs={{3,0},{2,1},{1,2},{0,3},{7,4},{6,5},{5,6},{4,7},{11,8},{10,9},{9,1... | collective-permute-start | bytes 6152 | tf_op jit(solution)/shard_map/ppermute | solution.py:342
  16.5 1.6 collective-permute-start.6
  20.0 5.0 %dispatch.1 = bf16[32,4,8,1536]{3,2,1,0:T(8,128)(2,1)} custom-call(s32[2]{0:T(128)S(1)} %pad_add_fusion.ids, s32[8,64]{1,0:T(8,128)S(1)} %bitcast.13, s32[8,64]{1,0:T(8,128)S(1)} %collective-permute-done.refs_1_, s32[8,64]{1,0:T(8,128)S(1)} %collective-permute-done.1.refs_2_, s32[8,64]{1,0:T(8,128)S(1)} %collective-permute-done.2.refs_3_, ...), custom_call_target="tpu_custom_call" | custom-call | tf_op jit(solution)/shard_map/dispatch/pallas_call | solution.py:347
  25.0 10.5 %all-to-all-start = ((bf16[32,32,1536]{2,1,0:T(8,128)(2,1)}), bf16[32,32,1536]{2,1,0:T(8,128)(2,1)S(1)}, u32[]{:S(2)}, u32[]{:S(2)}) async-start(bf16[32,32,1536]{2,1,0:T(8,128)(2,1)} %bitcast.4), calls=%async_computation | async-start | bytes 6291456 | tf_op jit(solution)/shard_map/all_to_all | solution.py:355
  35.5 1.4 collective-permute-start.13
  36.9 3.4 %shard_map.91 = (bf16[256,1536]{1,0:T(8,128)(2,1)}, bf16[256,1536]{1,0:T(8,128)(2,1)}, bf16[256,1536]{1,0:T(8,128)(2,1)}) custom-call(s32[2]{0:T(128)S(1)} %pad_add_fusion.ids, s32[128]{0:T(128)S(1)} %copy-done.3, s32[32]{0:T(128)S(1)} %copy-done.4, bf16[2,256,1536]{2,1,0:T(8,128)(2,1)} %own.2), custom_call_target="tpu_custom_call" | custom-call | tf_op jit(solution)/shard_map/pallas_call | solution.py:325
  40.3 1.9 collective-permute-start.7
  42.2 5.5 %collective-permute-start.8 = (bf16[256,1536]{1,0:T(8,128)(2,1)}, bf16[256,1536]{1,0:T(8,128)(2,1)S(1)}, u32[]{:S(2)}, u32[]{:S(2)}) collective-permute-start(bf16[256,1536]{1,0:T(8,128)(2,1)} %get-tuple-element.15), channel_id=1, source_target_pairs={{2,0},{3,1},{0,2},{1,3},{6,4},{7,5},{10,8},{11,9},{8,10},{9,11},{1... | collective-permute-start | bytes 2359304 | tf_op jit(solution)/shard_map/ppermute | solution.py:310
  47.8 2.1 collective-permute-start.9
  49.9 26.6 %collective-permute-done.6.refs_0_.swapped = bf16[2,256,1536]{2,1,0:T(8,128)(2,1)} collective-permute-done((bf16[2,256,1536]{2,1,0:T(8,128)(2,1)}, bf16[2,256,1536]{2,1,0:T(8,128)(2,1)}, u32[]{:S(2)}, u32[]{:S(2)}) %collective-permute-start.6) | collective-permute-done | bytes 1572896 | tf_op jit(solution)/shard_map/ppermute | solution.py:307
  76.5 2.9 %shard_map.92 = (bf16[256,1536]{1,0:T(8,128)(2,1)}, bf16[256,1536]{1,0:T(8,128)(2,1)}, bf16[256,1536]{1,0:T(8,128)(2,1)}) custom-call(s32[2]{0:T(128)S(1)} %pad_add_fusion.ids, s32[128]{0:T(128)S(1)} %copy-done.3, s32[32]{0:T(128)S(1)} %copy-done.4, bf16[2,256,1536]{2,1,0:T(8,128)(2,1)} %collective-permute-done.6.refs_0_.swapped), custom_call_target="tpu_custom_call" | custom-call | tf_op jit(solution)/shard_map/pallas_call | solution.py:313
  79.4 1.9 collective-permute-start.10
  81.3 20.4 %collective-permute-done.13.refs_1_.swapped = bf16[2,96,2048]{2,1,0:T(8,128)(2,1)S(1)} collective-permute-done((bf16[2,96,2048]{2,1,0:T(8,128)(2,1)}, bf16[2,96,2048]{2,1,0:T(8,128)(2,1)S(1)}, u32[]{:S(2)}, u32[]{:S(2)}) %collective-permute-start.13) | collective-permute-done | bytes 786464 | tf_op jit(solution)/shard_map/ppermute | solution.py:307
  102.6 3.5 %shard_map.93 = (bf16[2,96,2048]{2,1,0:T(8,128)(2,1)}, bf16[2,96,2048]{2,1,0:T(8,128)(2,1)}, bf16[2,96,2048]{2,1,0:T(8,128)(2,1)}) custom-call(s32[2]{0:T(128)S(1)} %pad_add_fusion.ids, s32[128]{0:T(128)S(1)} %copy-done.3, s32[32]{0:T(128)S(1)} %copy-done.4, bf16[2,96,2048]{2,1,0:T(8,128)(2,1)} %own.3, bf16[2,96,2048]{2,1,0:T(8,128)(2,1)} %copy-done.6), custom_call_target="tpu_custom_call" | custom-call | tf_op jit(solution)/shard_map/pallas_call | solution.py:325
  106.1 1.9 collective-permute-start.14
  108.0 3.4 %collective-permute-start.11 = (bf16[256,1536]{1,0:T(8,128)(2,1)}, bf16[256,1536]{1,0:T(8,128)(2,1)}, u32[]{:S(2)}, u32[]{:S(2)}) collective-permute-start(bf16[256,1536]{1,0:T(8,128)(2,1)} %get-tuple-element.18), channel_id=1, source_target_pairs={{2,0},{3,1},{0,2},{1,3},{6,4},{7,5},{10,8},{11,9},{8,10},{9,11},{1... | collective-permute-start | bytes 2359304 | tf_op jit(solution)/shard_map/ppermute | solution.py:310
  111.4 4.3 %collective-permute-start.12 = (bf16[256,1536]{1,0:T(8,128)(2,1)}, bf16[256,1536]{1,0:T(8,128)(2,1)}, u32[]{:S(2)}, u32[]{:S(2)}) collective-permute-start(bf16[256,1536]{1,0:T(8,128)(2,1)} %get-tuple-element.19), channel_id=1, source_target_pairs={{3,0},{2,1},{1,2},{0,3},{7,4},{6,5},{11,8},{10,9},{9,10},{8,11},{1... | collective-permute-start | bytes 2359304 | tf_op jit(solution)/shard_map/ppermute | solution.py:310
  115.7 1.9 collective-permute-start.15
  118.6 3.1 %collective-permute-start.16 = (bf16[2,96,2048]{2,1,0:T(8,128)(2,1)}, bf16[2,96,2048]{2,1,0:T(8,128)(2,1)}, u32[]{:S(2)}, u32[]{:S(2)}) collective-permute-start(bf16[2,96,2048]{2,1,0:T(8,128)(2,1)} %get-tuple-element.22), channel_id=1, source_target_pairs={{3,0},{2,1},{1,2},{0,3},{7,4},{6,5},{11,8},{10,9},{9,10},{8,11},{1... | collective-permute-start | bytes 2359304 | tf_op jit(solution)/shard_map/ppermute | solution.py:310
  123.0 18.8 %collective-permute-done.11.refs_4_ = bf16[256,1536]{1,0:T(8,128)(2,1)} collective-permute-done((bf16[256,1536]{1,0:T(8,128)(2,1)}, bf16[256,1536]{1,0:T(8,128)(2,1)}, u32[]{:S(2)}, u32[]{:S(2)}) %collective-permute-start.11) | collective-permute-done | bytes 786464 | tf_op jit(solution)/shard_map/ppermute | solution.py:310
  141.8 22.8 %collective-permute-done.12.refs_5_ = bf16[256,1536]{1,0:T(8,128)(2,1)} collective-permute-done((bf16[256,1536]{1,0:T(8,128)(2,1)}, bf16[256,1536]{1,0:T(8,128)(2,1)}, u32[]{:S(2)}, u32[]{:S(2)}) %collective-permute-start.12) | collective-permute-done | bytes 786464 | tf_op jit(solution)/shard_map/ppermute | solution.py:310
  164.7 7.6 %up.1.h = bf16[768,768]{1,0:T(8,128)(2,1)S(1)} custom-call(s32[2]{0:T(128)S(1)} %pad_add_fusion.ids, s32[128]{0:T(128)S(1)} %copy-done.3, s32[32]{0:T(128)S(1)} %copy-done.4, bf16[768,2048]{1,0:T(8,128)(2,1)S(1)} %compact.1.x, bf16[2,256,1536]{2,1,0:T(8,128)(2,1)} %own.2, bf16[2,256,1536]{2,1,0:T(8,128)(2,1)} %collective-permute-done.6.refs_0_.swapped, ...), custom_call_target="tpu_custom_call" | custom-call | tf_op jit(solution)/shard_map/up/pallas_call | solution.py:382
  172.3 9.2 %collective-permute-done.16.refs_2_ = bf16[2,96,2048]{2,1,0:T(8,128)(2,1)} collective-permute-done((bf16[2,96,2048]{2,1,0:T(8,128)(2,1)}, bf16[2,96,2048]{2,1,0:T(8,128)(2,1)}, u32[]{:S(2)}, u32[]{:S(2)}) %collective-permute-start.16) | collective-permute-done | bytes 786464 | tf_op jit(solution)/shard_map/ppermute | solution.py:310
  181.5 7.2 %down.1 = bf16[1024,1536]{1,0:T(8,128)(2,1)} custom-call(s32[2]{0:T(128)S(1)} %pad_add_fusion.ids, s32[128]{0:T(128)S(1)} %copy-done.3, s32[32]{0:T(128)S(1)} %copy-done.4, bf16[768,768]{1,0:T(8,128)(2,1)S(1)} %up.1.h, bf16[2,96,2048]{2,1,0:T(8,128)(2,1)} %own.3, bf16[2,96,2048]{2,1,0:T(8,128)(2,1)} %copy-done.6, ...), custom_call_target="tpu_custom_call" | custom-call | tf_op jit(solution)/shard_map/down/pallas_call | solution.py:391
  188.7 13.0 %all-to-all-start.1 = ((bf16[128,8,1536]{2,1,0:T(8,128)(2,1)}), bf16[128,8,1536]{2,1,0:T(8,128)(2,1)S(1)}, u32[]{:S(2)}, u32[]{:S(2)}) async-start(bf16[128,8,1536]{2,1,0:T(8,128)(2,1)} %bitcast.16), calls=%async_computation.1 | async-start | bytes 6291456 | tf_op jit(solution)/shard_map/all_to_all | solution.py:406
  201.7 2.0 weigh.1.weight
  203.7 39.6 %all-to-all-done.1 = bf16[128,8,1536]{2,1,0:T(8,128)(2,1)S(1)} async-done(((bf16[128,8,1536]{2,1,0:T(8,128)(2,1)}), bf16[128,8,1536]{2,1,0:T(8,128)(2,1)S(1)}, u32[]{:S(2)}, u32[]{:S(2)}) %all-to-all-start.1) | async-done | bytes 3145760 | tf_op jit(solution)/shard_map/all_to_all | solution.py:406
  243.3 2.9 %combine.1 = bf16[64,2048]{1,0:T(8,128)(2,1)} custom-call(bf16[4,128,1024]{2,1,0:T(8,128)(2,1)} %weigh.1.weight, bf16[1024,1536]{1,0:T(8,128)(2,1)S(1)} %bitcast.9), custom_call_target="tpu_custom_call" | custom-call | tf_op jit(solution)/shard_map/combine/pallas_call | solution.py:410
  (38 shorter events, 5.2 us)
Async XLA Ops:
  0.0 18.3 %collective-permute-start.3 = (bf16[64,2048]{1,0:T(8,128)(2,1)}, bf16[64,2048]{1,0:T(8,128)(2,1)S(1)}, u32[]{:S(2)}, u32[]{:S(2)}) collective-permute-start(bf16[64,2048]{1,0:T(8,128)(2,1)} %refs_4_.1), channel_id=1, source_target_pairs={{1,0},{0,1},{3,2},{2,3},{5,4},{4,5},{7,6},{6,7},{9,8},{8,9},{11,10... | collective-permute-start | bytes 786440 | tf_op jit(solution)/shard_map/ppermute | solution.py:341
  2.0 16.3 %collective-permute-start.4 = (bf16[64,2048]{1,0:T(8,128)(2,1)}, bf16[64,2048]{1,0:T(8,128)(2,1)S(1)}, u32[]{:S(2)}, u32[]{:S(2)}) collective-permute-start(bf16[64,2048]{1,0:T(8,128)(2,1)} %refs_4_.1), channel_id=1, source_target_pairs={{2,0},{3,1},{0,2},{1,3},{6,4},{7,5},{4,6},{5,7},{10,8},{11,9},{8,1... | collective-permute-start | bytes 786440 | tf_op jit(solution)/shard_map/ppermute | solution.py:341
  4.5 13.8 %collective-permute-start.5 = (bf16[64,2048]{1,0:T(8,128)(2,1)}, bf16[64,2048]{1,0:T(8,128)(2,1)S(1)}, u32[]{:S(2)}, u32[]{:S(2)}) collective-permute-start(bf16[64,2048]{1,0:T(8,128)(2,1)} %refs_4_.1), channel_id=1, source_target_pairs={{3,0},{2,1},{1,2},{0,3},{7,4},{6,5},{5,6},{4,7},{11,8},{10,9},{9,1... | collective-permute-start | bytes 786440 | tf_op jit(solution)/shard_map/ppermute | solution.py:341
  4.5 9.1 %collective-permute-start = (s32[8,64]{1,0:T(8,128)}, s32[8,64]{1,0:T(8,128)S(1)}, u32[]{:S(2)}, u32[]{:S(2)}) collective-permute-start(s32[8,64]{1,0:T(8,128)} %bitcast.10), channel_id=1, source_target_pairs={{1,0},{0,1},{3,2},{2,3},{5,4},{4,5},{7,6},{6,7},{9,8},{8,9},{11,10... | collective-permute-start | bytes 6152 | tf_op jit(solution)/shard_map/ppermute | solution.py:342
  4.7 11.8 %collective-permute-start.1 = (s32[8,64]{1,0:T(8,128)}, s32[8,64]{1,0:T(8,128)S(1)}, u32[]{:S(2)}, u32[]{:S(2)}) collective-permute-start(s32[8,64]{1,0:T(8,128)} %bitcast.11), channel_id=1, source_target_pairs={{2,0},{3,1},{0,2},{1,3},{6,4},{7,5},{4,6},{5,7},{10,8},{11,9},{8,1... | collective-permute-start | bytes 6152 | tf_op jit(solution)/shard_map/ppermute | solution.py:342
  13.6 4.7 %collective-permute-start.2 = (s32[8,64]{1,0:T(8,128)}, s32[8,64]{1,0:T(8,128)S(1)}, u32[]{:S(2)}, u32[]{:S(2)}) collective-permute-start(s32[8,64]{1,0:T(8,128)} %bitcast.12), channel_id=1, source_target_pairs={{3,0},{2,1},{1,2},{0,3},{7,4},{6,5},{5,6},{4,7},{11,8},{10,9},{9,1... | collective-permute-start | bytes 6152 | tf_op jit(solution)/shard_map/ppermute | solution.py:342
  16.5 60.0 %collective-permute-start.6 = (bf16[2,256,1536]{2,1,0:T(8,128)(2,1)}, bf16[2,256,1536]{2,1,0:T(8,128)(2,1)}, u32[]{:S(2)}, u32[]{:S(2)}) collective-permute-start(bf16[2,256,1536]{2,1,0:T(8,128)(2,1)} %own.2), channel_id=1, source_target_pairs={{0,4},{4,0},{1,5},{5,1},{2,6},{6,2},{3,7},{7,3},{8,12},{12,8},{9,1... | collective-permute-start | bytes 4718600 | tf_op jit(solution)/shard_map/ppermute | solution.py:307
  18.3 1.0 copy-start
  19.3 0.7 copy-start.1
  25.0 11.9 %copy-start.3 = (s32[128]{0:T(128)S(1)}, s32[128]{0:T(128)}, u32[]{:S(2)}) copy-start(s32[128]{0:T(128)} %table.9) | copy-start | bytes 1540
  25.0 11.9 %copy-start.4 = (s32[32]{0:T(128)S(1)}, s32[32]{0:T(128)}, u32[]{:S(2)}) copy-start(s32[32]{0:T(128)} %refreshed.9) | copy-start | bytes 388
  25.0 96.7 %all-to-all-start = ((bf16[32,32,1536]{2,1,0:T(8,128)(2,1)}), bf16[32,32,1536]{2,1,0:T(8,128)(2,1)S(1)}, u32[]{:S(2)}, u32[]{:S(2)}) async-start(bf16[32,32,1536]{2,1,0:T(8,128)(2,1)} %bitcast.4), calls=%async_computation | async-start | bytes 6291456 | tf_op jit(solution)/shard_map/all_to_all | solution.py:355
  35.5 66.2 %collective-permute-start.13 = (bf16[2,96,2048]{2,1,0:T(8,128)(2,1)}, bf16[2,96,2048]{2,1,0:T(8,128)(2,1)S(1)}, u32[]{:S(2)}, u32[]{:S(2)}) collective-permute-start(bf16[2,96,2048]{2,1,0:T(8,128)(2,1)} %own.3), channel_id=1, source_target_pairs={{0,4},{4,0},{1,5},{5,1},{2,6},{6,2},{3,7},{7,3},{8,12},{12,8},{9,1... | collective-permute-start | bytes 2359304 | tf_op jit(solution)/shard_map/ppermute | solution.py:307
  40.3 67.7 %collective-permute-start.7 = (bf16[256,1536]{1,0:T(8,128)(2,1)}, bf16[256,1536]{1,0:T(8,128)(2,1)S(1)}, u32[]{:S(2)}, u32[]{:S(2)}) collective-permute-start(bf16[256,1536]{1,0:T(8,128)(2,1)} %get-tuple-element.14), channel_id=1, source_target_pairs={{1,0},{0,1},{3,2},{2,3},{5,4},{4,5},{9,8},{8,9},{11,10},{10,11},{1... | collective-permute-start | bytes 2359304 | tf_op jit(solution)/shard_map/ppermute | solution.py:310
  42.2 69.2 %collective-permute-start.8 = (bf16[256,1536]{1,0:T(8,128)(2,1)}, bf16[256,1536]{1,0:T(8,128)(2,1)S(1)}, u32[]{:S(2)}, u32[]{:S(2)}) collective-permute-start(bf16[256,1536]{1,0:T(8,128)(2,1)} %get-tuple-element.15), channel_id=1, source_target_pairs={{2,0},{3,1},{0,2},{1,3},{6,4},{7,5},{10,8},{11,9},{8,10},{9,11},{1... | collective-permute-start | bytes 2359304 | tf_op jit(solution)/shard_map/ppermute | solution.py:310
  47.8 67.9 %collective-permute-start.9 = (bf16[256,1536]{1,0:T(8,128)(2,1)}, bf16[256,1536]{1,0:T(8,128)(2,1)S(1)}, u32[]{:S(2)}, u32[]{:S(2)}) collective-permute-start(bf16[256,1536]{1,0:T(8,128)(2,1)} %get-tuple-element.16), channel_id=1, source_target_pairs={{3,0},{2,1},{1,2},{0,3},{7,4},{6,5},{11,8},{10,9},{9,10},{8,11},{1... | collective-permute-start | bytes 2359304 | tf_op jit(solution)/shard_map/ppermute | solution.py:310
  79.4 38.3 %collective-permute-start.10 = (bf16[256,1536]{1,0:T(8,128)(2,1)}, bf16[256,1536]{1,0:T(8,128)(2,1)S(1)}, u32[]{:S(2)}, u32[]{:S(2)}) collective-permute-start(bf16[256,1536]{1,0:T(8,128)(2,1)} %get-tuple-element.17), channel_id=1, source_target_pairs={{1,0},{0,1},{3,2},{2,3},{5,4},{4,5},{9,8},{8,9},{11,10},{10,11},{1... | collective-permute-start | bytes 2359304 | tf_op jit(solution)/shard_map/ppermute | solution.py:310
  101.7 0.9 copy-start.6
  106.1 66.2 %collective-permute-start.14 = (bf16[2,96,2048]{2,1,0:T(8,128)(2,1)}, bf16[2,96,2048]{2,1,0:T(8,128)(2,1)}, u32[]{:S(2)}, u32[]{:S(2)}) collective-permute-start(bf16[2,96,2048]{2,1,0:T(8,128)(2,1)} %get-tuple-element.20), channel_id=1, source_target_pairs={{1,0},{0,1},{3,2},{2,3},{5,4},{4,5},{9,8},{8,9},{11,10},{10,11},{1... | collective-permute-start | bytes 2359304 | tf_op jit(solution)/shard_map/ppermute | solution.py:310
  108.0 9.7 %copy-start.7 = (bf16[256,1536]{1,0:T(8,128)(2,1)}, bf16[256,1536]{1,0:T(8,128)(2,1)S(1)}, u32[]{:S(2)}) copy-start(bf16[256,1536]{1,0:T(8,128)(2,1)S(1)} %collective-permute-done.7.refs_0_) | copy-start | bytes 2359300
  108.0 33.8 %collective-permute-start.11 = (bf16[256,1536]{1,0:T(8,128)(2,1)}, bf16[256,1536]{1,0:T(8,128)(2,1)}, u32[]{:S(2)}, u32[]{:S(2)}) collective-permute-start(bf16[256,1536]{1,0:T(8,128)(2,1)} %get-tuple-element.18), channel_id=1, source_target_pairs={{2,0},{3,1},{0,2},{1,3},{6,4},{7,5},{10,8},{11,9},{8,10},{9,11},{1... | collective-permute-start | bytes 2359304 | tf_op jit(solution)/shard_map/ppermute | solution.py:310
  111.4 6.3 %copy-start.8 = (bf16[256,1536]{1,0:T(8,128)(2,1)}, bf16[256,1536]{1,0:T(8,128)(2,1)S(1)}, u32[]{:S(2)}) copy-start(bf16[256,1536]{1,0:T(8,128)(2,1)S(1)} %collective-permute-done.8.refs_1_) | copy-start | bytes 2359300
  111.4 53.2 %collective-permute-start.12 = (bf16[256,1536]{1,0:T(8,128)(2,1)}, bf16[256,1536]{1,0:T(8,128)(2,1)}, u32[]{:S(2)}, u32[]{:S(2)}) collective-permute-start(bf16[256,1536]{1,0:T(8,128)(2,1)} %get-tuple-element.19), channel_id=1, source_target_pairs={{3,0},{2,1},{1,2},{0,3},{7,4},{6,5},{11,8},{10,9},{9,10},{8,11},{1... | collective-permute-start | bytes 2359304 | tf_op jit(solution)/shard_map/ppermute | solution.py:310
  115.7 2.0 copy-start.9
  115.7 56.6 %collective-permute-start.15 = (bf16[2,96,2048]{2,1,0:T(8,128)(2,1)}, bf16[2,96,2048]{2,1,0:T(8,128)(2,1)}, u32[]{:S(2)}, u32[]{:S(2)}) collective-permute-start(bf16[2,96,2048]{2,1,0:T(8,128)(2,1)} %get-tuple-element.21), channel_id=1, source_target_pairs={{2,0},{3,1},{0,2},{1,3},{6,4},{7,5},{10,8},{11,9},{8,10},{9,11},{1... | collective-permute-start | bytes 2359304 | tf_op jit(solution)/shard_map/ppermute | solution.py:310
  117.7 0.9 copy-start.10
  118.6 62.9 %collective-permute-start.16 = (bf16[2,96,2048]{2,1,0:T(8,128)(2,1)}, bf16[2,96,2048]{2,1,0:T(8,128)(2,1)}, u32[]{:S(2)}, u32[]{:S(2)}) collective-permute-start(bf16[2,96,2048]{2,1,0:T(8,128)(2,1)} %get-tuple-element.22), channel_id=1, source_target_pairs={{3,0},{2,1},{1,2},{0,3},{7,4},{6,5},{11,8},{10,9},{9,10},{8,11},{1... | collective-permute-start | bytes 2359304 | tf_op jit(solution)/shard_map/ppermute | solution.py:310
  188.7 13.0 %copy-start.2 = (s32[64,8]{0,1:T(8,128)S(1)}, s32[64,8]{0,1:T(8,128)}, u32[]{:S(2)}) copy-start(s32[64,8]{0,1:T(8,128)} %param.10) | copy-start | bytes 6148
  188.7 13.0 %copy-start.5 = (f32[64,8]{0,1:T(8,128)S(1)}, f32[64,8]{0,1:T(8,128)}, u32[]{:S(2)}) copy-start(f32[64,8]{0,1:T(8,128)} %param.11) | copy-start | bytes 6148
  188.7 54.6 %all-to-all-start.1 = ((bf16[128,8,1536]{2,1,0:T(8,128)(2,1)}), bf16[128,8,1536]{2,1,0:T(8,128)(2,1)S(1)}, u32[]{:S(2)}, u32[]{:S(2)}) async-start(bf16[128,8,1536]{2,1,0:T(8,128)(2,1)} %bitcast.16), calls=%async_computation.1 | async-start | bytes 6291456 | tf_op jit(solution)/shard_map/all_to_all | solution.py:406
